TPU v7x, 32 devices: a whole 2x2x4 slice. The times are simulated.
32 devices in a mesh: seq: 8 (over z, x), head: 4 (over y, core).
Axes of the slice: x: 2, y: 2, z: 4, core: 2. Of those that a mesh axis runs over, the one named last changes fastest.
Arguments:
- token_ids: int32 [8192], P('seq'), may hold values from 0 to 255
- embedding: bfloat16 [256, 1024], replicated, may hold values from -6 to 6
- fine_norm: float32 [1024], replicated, may hold values from 0.1 to 1.9
- fine_query: bfloat16 [1024, 1024], P(None, 'head'), may hold values from -2 to 2
- fine_key: bfloat16 [1024, 1024], P(None, 'head'), may hold values from -2 to 2
- fine_value: bfloat16 [1024, 1024], P(None, 'head'), may hold values from -0.1875 to 0.1875
- fine_output: bfloat16 [1024, 1024], P('head'), may hold values from -0.1875 to 0.1875
- shorten_weight: bfloat16 [4, 1024, 1024], P(None, 'head'), may hold values from -0.09375 to 0.09375
- coarse_norm: float32 [1024], replicated, may hold values from 0.1 to 1.9
- coarse_query: bfloat16 [1024, 1024], P(None, 'head'), may hold values from -2 to 2
- coarse_key: bfloat16 [1024, 1024], P(None, 'head'), may hold values from -2 to 2
- coarse_value: bfloat16 [1024, 1024], P(None, 'head'), may hold values from -0.1875 to 0.1875
- coarse_output: bfloat16 [1024, 1024], P('head'), may hold values from -0.1875 to 0.1875
- ffn_norm: float32 [1024], replicated, may hold values from 0.1 to 1.9
- ffn_up: bfloat16 [1024, 4096], P(None, 'head'), may hold values from -0.1875 to 0.1875
- ffn_down: bfloat16 [4096, 1024], P('head'), may hold values from -0.09375 to 0.09375
- upsample_weight: bfloat16 [1024, 4, 1024], P(None, None, 'head'), may hold values from -0.1875 to 0.1875
Outputs:
- block_output: bfloat16 [8192, 1024], P('seq', 'head')
All inputs are finite; a program needn't handle non-finite values.
Results may differ from a plain program's by a relative error of at most 0.0102.
Values may be sent and summed in bfloat16 or wider, within the bound.
A program may use at most 128 MiB of HBM per device.

v0:
```python
import math

import jax
import jax.numpy as jnp
from jax import lax
from jax.experimental import pallas as pl
from jax.experimental.pallas import tpu as pltpu
from jax.sharding import PartitionSpec as P

D = 1024
HEAD_DIM = 64
HALF = HEAD_DIM // 2
SHORTEN = 4
WINDOW = 1024
LEAD = 128
CARRY = 16

epsilon = 1e-06
masked_low = -1e30
MESH = pl.DeviceIdType.MESH
EXP2_SCALE = HEAD_DIM ** (-0.5) * math.log2(math.e)
VMEM_SPEC = pl.BlockSpec(memory_space=pltpu.VMEM)
ANY_SPEC = pl.BlockSpec(memory_space=pl.ANY)

RELAY, FINISH, MIDDLE, TOTAL, PROJECT, FORWARD = (2, 3, 4, 5, 6, 8)
STEP_KEYS = 512
PIECES = 2


def dot(left, right):
    return jnp.dot(left, right, preferred_element_type=jnp.float32)


def dot_nt(left, right):
    return lax.dot_general(left, right, (((1,), (1,)), ((), ())), preferred_element_type=jnp.float32)


def dot_tn(left, right):
    return lax.dot_general(left, right, (((0,), (0,)), ((), ())), preferred_element_type=jnp.float32)


def normed(data, gain):
    power = jnp.mean(data * data, axis=1, keepdims=True)
    return (data * lax.rsqrt(power + epsilon) * gain).astype(jnp.bfloat16)


def aligned(start, size, unit):
    return pl.ds(pl.multiple_of(start, unit), size)


def periods(column):
    log = 4 + lax.shift_right_logical(column * 14, 5)
    return jnp.left_shift(jnp.ones_like(log), log)


def phase(position, period):
    cycle = jnp.bitwise_and(position, period - 1).astype(jnp.float32)
    return cycle * (2.0 * math.pi / period.astype(jnp.float32))


def remote(source, target, send, receive, device):
    return pltpu.make_async_remote_copy(
        src_ref=source, dst_ref=target, send_sem=send, recv_sem=receive, device_id=device, device_id_type=MESH
    )


class HeadSum:
    def __init__(self, index, peers, part, out, buffers, send_sem, recv_sem):
        self.index = index
        self.me, self.sibling, self.across = peers
        self.part, self.out = part, out
        self.send_a, self.recv_a, self.send_b, self.recv_b, self.final = (buffer.at[index] for buffer in buffers)
        self.send_sem, self.recv_sem = send_sem, recv_sem
        half = part.shape[1] // 2
        self.mine = aligned((self.me % 2) * half, half, half)
        self.theirs = aligned((self.sibling % 2) * half, half, half)

    def copy(self, kind, piece, source, target, device):
        return remote(
            source, target, self.send_sem.at[self.index, kind, piece], self.recv_sem.at[self.index, kind, piece],
            {"head": device},
        )

    def copy_a(self, piece, at):
        return self.copy(0, piece, self.send_a.at[at, :], self.recv_a.at[at, :], self.sibling)

    def copy_b(self, piece, at):
        return self.copy(1, piece, self.send_b.at[at, :], self.recv_b.at[at, :], self.across)

    def copy_c(self, piece, at):
        return self.copy(2, piece, self.final.at[at, :], self.out.at[at, self.mine], self.sibling)

    def begin(self, piece, at):
        self.send_a[at, :] = self.part[at, self.theirs].astype(jnp.bfloat16)
        self.copy_a(piece, at).start()

    def middle(self, piece, at):
        self.copy_a(piece, at).wait_recv()
        summed = self.part[at, self.mine] + self.recv_a[at, :].astype(jnp.float32)
        self.part[at, self.mine] = summed
        self.send_b[at, :] = summed.astype(jnp.bfloat16)
        self.copy_b(piece, at).start()

    def total(self, piece, at, residual=None):
        self.copy_b(piece, at).wait_recv()
        value = self.part[at, self.mine] + self.recv_b[at, :].astype(jnp.float32)
        if residual is not None:
            value = value + residual[at, self.mine]
        value = value.astype(jnp.bfloat16)
        self.final[at, :] = value
        self.copy_c(piece, at).start()
        self.out[at, self.mine] = value

    def end(self, piece, at):
        self.copy_c(piece, at).wait_recv()

    def drain(self, piece, at):
        self.copy_a(piece, at).wait_send()
        self.copy_b(piece, at).wait_send()
        self.copy_c(piece, at).wait_send()


def scratch_list(count, width, chunks, places):
    full = 4 * width
    rows = count // SHORTEN
    frame = LEAD + WINDOW + count
    low = jnp.bfloat16
    wide = jnp.float32
    dma = pltpu.SemaphoreType.DMA
    return [
        ("emb", pltpu.VMEM((256, full), low)),
        ("fq", pltpu.VMEM((full, width), low)),
        ("fk", pltpu.VMEM((full, width), low)),
        ("fv", pltpu.VMEM((full, width), low)),
        ("cols", pltpu.VMEM((full, width), low)),
        ("ws", pltpu.VMEM((SHORTEN, width, full), low)),
        ("cq", pltpu.VMEM((full, width), low)),
        ("ck", pltpu.VMEM((full, width), low)),
        ("cv", pltpu.VMEM((full, width), low)),
        ("co", pltpu.VMEM((width, full), low)),
        ("up", pltpu.VMEM((full, full), low)),
        ("down", pltpu.VMEM((full, full), low)),
        ("lift", pltpu.VMEM((full, SHORTEN * width), low)),
        ("load_sem", dma((13,))),
        ("ids", pltpu.VMEM((1, frame), jnp.int32)),
        ("id_send", dma((2,))),
        ("id_recv", dma((2,))),
        ("col_send", dma((4,))),
        ("col_recv", dma((4,))),
        ("tabs", pltpu.VMEM((6, 256, width), low)),
        ("cos_t", pltpu.VMEM((HALF, frame), wide)),
        ("sin_t", pltpu.VMEM((HALF, frame), wide)),
        ("keys", pltpu.VMEM((width, frame), low)),
        ("values", pltpu.VMEM((width, frame), low)),
        ("query", pltpu.VMEM((LEAD + count, width), low)),
        ("start", pltpu.VMEM((LEAD + count, width), low)),
        ("mixed", pltpu.VMEM((CARRY + count, width), low)),
        ("others", pltpu.VMEM((CARRY + count, 3 * width), low)),
        ("mix_send", dma((3, chunks + 1))),
        ("mix_recv", dma((3, chunks + 1))),
        ("stream", pltpu.VMEM((width // 128, CARRY + count, 128), wide)),
        ("part", pltpu.VMEM((rows, full), wide)),
        ("part_b", pltpu.VMEM((rows, full), wide)),
        ("short", pltpu.VMEM((rows, full), low)),
        ("summed", pltpu.VMEM((rows, full), low)),
        ("first", pltpu.VMEM((rows, full), wide)),
        ("second", pltpu.VMEM((rows, full), low)),
        ("send_a", pltpu.VMEM((3, rows, full // 2), low)),
        ("recv_a", pltpu.VMEM((3, rows, full // 2), low)),
        ("send_b", pltpu.VMEM((3, rows, full // 2), low)),
        ("recv_b", pltpu.VMEM((3, rows, full // 2), low)),
        ("final", pltpu.VMEM((3, rows, full // 2), low)),
        ("sum_send", dma((3, 3, chunks))),
        ("sum_recv", dma((3, 3, chunks))),
        ("coarse_cos", pltpu.VMEM((rows, width), wide)),
        ("coarse_sin", pltpu.VMEM((rows, width), wide)),
        ("pair_out", pltpu.VMEM((2, rows, width), low)),
        ("query_out", pltpu.VMEM((2, rows, width // 2), low)),
        ("pairs", pltpu.VMEM((places * rows, width), low)),
        ("queries", pltpu.VMEM((2 * rows, width // 2), low)),
        ("pair_send", dma((places, chunks))),
        ("pair_recv", dma((places, chunks))),
        ("query_send", dma((chunks,))),
        ("query_recv", dma((chunks,))),
        ("top", pltpu.VMEM((2, 2 * rows, 1), wide)),
        ("norm", pltpu.VMEM((2, 2 * rows, 1), wide)),
        ("acc", pltpu.VMEM((2, 2 * rows, width // 2), wide)),
        ("turn", pltpu.VMEM((rows, width // 2), low)),
        ("heads_in", pltpu.VMEM((rows, width), low)),
        ("turn_send", dma((1,))),
        ("turn_recv", dma((1,))),
        ("spread", pltpu.VMEM((width // 128, count, 128), wide)),
    ]


class Names:
    pass


def block_kernel(names, chunk_rows, *refs):
    (ids_ref, fine_gain, coarse_gain, ffn_gain, emb_h, fq_h, fk_h, fv_h, fo_h, ws_h,
     cq_h, ck_h, cv_h, co_h, up_h, down_h, lift_h, out_ref) = refs[:18]
    s = Names()
    for name, ref in zip(names, refs[18:]):
        setattr(s, name, ref)
    count, width = out_ref.shape
    full = 4 * width
    heads = width // HEAD_DIM
    chunks = count // chunk_rows
    group = chunk_rows // SHORTEN
    rows = count // SHORTEN
    frame = LEAD + WINDOW + count
    span = WINDOW + chunk_rows
    lanes = width // 128
    pair = width // 2

    places = lax.axis_size("seq")
    place = lax.axis_index("seq")
    levels = places // 2
    side = place % 2
    level = place // 2
    cross = place + 1 - 2 * side
    me = lax.axis_index("head")
    sibling = me + 1 - 2 * (me % 2)
    across = (me + 2) % 4
    diagonal = (sibling + 2) % 4

    barrier = pltpu.get_barrier_semaphore()
    for device in (sibling, across, diagonal):
        pl.semaphore_signal(barrier, inc=1, device_id={"head": device}, device_id_type=MESH)

    def greet(step, state):
        pl.semaphore_signal(
            barrier, inc=1, device_id={"seq": (place + step) % places}, device_id_type=MESH
        )
        return state

    lax.fori_loop(1, places, greet, 0)

    own_columns = aligned(me * width, width, width)
    loads = {
        name: pltpu.make_async_copy(source, target, s.load_sem.at[index])
        for index, (name, source, target) in enumerate((
            ("emb", emb_h, s.emb), ("fk", fk_h, s.fk), ("fv", fv_h, s.fv), ("fq", fq_h, s.fq),
            ("cols", fo_h.at[:, own_columns], s.cols.at[pl.ds(0, width), :]),
            ("ws", ws_h, s.ws), ("cq", cq_h, s.cq), ("ck", ck_h, s.ck), ("cv", cv_h, s.cv), ("co", co_h, s.co),
            ("up", up_h, s.up), ("down", down_h, s.down), ("lift", lift_h, s.lift),
        ))
    }
    for load in loads.values():
        load.start()

    s.ids[:, LEAD + WINDOW :] = ids_ref[...]

    @pl.when(place < 1)
    def _():
        s.ids[:, LEAD : LEAD + WINDOW] = jnp.zeros((1, WINDOW), jnp.int32)

    @pl.when(place < 2)
    def _():
        s.ids[:, :LEAD] = jnp.zeros((1, LEAD), jnp.int32)

    def clear(index, state):
        chunk = index // (places - 2)
        blank = index % (places - 2)

        @pl.when(blank + 2 >= 2 * level + 2)
        def _():
            at = aligned((chunk * places + blank + 2) * group, group, group)
            s.pairs[at, :] = jnp.zeros((group, width), jnp.bfloat16)

        return state

    lax.fori_loop(0, chunks * (places - 2), clear, 0)

    column = lax.broadcasted_iota(jnp.int32, (HALF, 128), 0)
    lane = lax.broadcasted_iota(jnp.int32, (HALF, 128), 1)
    period = periods(column)
    small = phase(lane, period)
    base = (place - 1) * count - LEAD
    large = phase(base + 128 * lane, period)
    cos_b, sin_b, cos_a, sin_a = jnp.cos(small), jnp.sin(small), jnp.cos(large), jnp.sin(large)
    for block in range(frame // 128):
        at = slice(block * 128, block * 128 + 128)
        cos_k, sin_k = cos_a[:, block : block + 1], sin_a[:, block : block + 1]
        s.cos_t[:, at] = cos_b * cos_k - sin_b * sin_k
        s.sin_t[:, at] = sin_b * cos_k + cos_b * sin_k

    pl.semaphore_wait(barrier, places + 2)

    def id_copy(steps):
        if steps == 1:
            target = s.ids.at[:, pl.ds(LEAD, WINDOW)]
            source = ids_ref
        else:
            target = s.ids.at[:, pl.ds(0, LEAD)]
            source = ids_ref.at[:, pl.ds(count - LEAD, LEAD)]
        device = (place + steps) % places
        return remote(source, target, s.id_send.at[steps - 1], s.id_recv.at[steps - 1], {"seq": device})

    for steps in (1, 2):
        @pl.when(place + steps < places)
        def _():
            id_copy(steps).start()

    def column_copy(flip, device):
        return remote(
            fo_h.at[:, aligned(device * width, width, width)], s.cols.at[pl.ds(flip * width, width), :],
            s.col_send.at[flip], s.col_recv.at[flip], {"head": device},
        )

    column_copies = [column_copy(flip, device) for flip, device in ((1, sibling), (2, across), (3, diagonal))]
    for copy in column_copies:
        copy.start()

    loads["emb"].wait()
    level_in = normed(s.emb[...].astype(jnp.float32), fine_gain[...])

    def split(values):
        high = values.astype(jnp.bfloat16)
        return high, (values - high.astype(jnp.float32)).astype(jnp.bfloat16)

    loads["fk"].wait()
    s.tabs[0], s.tabs[1] = split(dot(level_in, s.fk[...]).T)
    loads["fv"].wait()
    s.tabs[2] = dot(level_in, s.fv[...]).T.astype(jnp.bfloat16)
    loads["fq"].wait()
    s.tabs[3], s.tabs[4] = split(dot(level_in, s.fq[...]).T)
    s.tabs[5] = s.emb[:, own_columns]

    for steps in (1, 2):
        @pl.when(place >= steps)
        def _():
            id_copy(steps).wait_recv()

    def turned(joined, at):
        cosine, sine = s.cos_t[:, at], s.sin_t[:, at]
        pieces = []
        for head in range(heads):
            low = joined[head * HEAD_DIM : head * HEAD_DIM + HALF]
            high = joined[head * HEAD_DIM + HALF : (head + 1) * HEAD_DIM]
            pieces += [low * cosine - high * sine, high * cosine + low * sine]
        return jnp.concatenate(pieces, axis=0)

    def token_rows(begin, size, queries):
        at = aligned(begin, size, 128)
        levels_at = lax.broadcasted_iota(jnp.int32, (256, size), 0)
        hot = jnp.where(levels_at == s.ids[:, at], 1.0, 0.0).astype(jnp.bfloat16)
        s.keys[:, at] = turned(dot(s.tabs[0], hot) + dot(s.tabs[1], hot), at).astype(jnp.bfloat16)
        s.values[:, at] = dot(s.tabs[2], hot).astype(jnp.bfloat16)
        if queries:
            to = aligned(begin - WINDOW, size, 128)
            turned_q = turned(dot(s.tabs[3], hot) + dot(s.tabs[4], hot), at)
            s.query[to, :] = turned_q.T.astype(jnp.bfloat16)
            s.start[to, :] = dot_tn(hot, s.tabs[5]).astype(jnp.bfloat16)

    early = 256
    late = (LEAD + count) // 3

    def early_rows(index, state):
        token_rows(index * early, early, False)
        return state

    def late_rows(index, state):
        token_rows(WINDOW + index * late, late, True)
        return state

    lax.fori_loop(0, WINDOW // early, early_rows, 0)
    lax.fori_loop(0, 3, late_rows, 0)

    def attend(query, key_at, mask):
        size = query.shape[0]
        lane_head = lax.broadcasted_iota(jnp.int32, (size, width), 1) // HEAD_DIM
        result = jnp.zeros((size, width), jnp.float32)
        for head in range(heads):
            masked_q = jnp.where(lane_head == head, query, jnp.zeros_like(query))
            pieces = mask(dot(masked_q, s.keys[:, key_at]))
            top = pieces[0]
            for piece in pieces[1:]:
                top = jnp.maximum(top, piece)
            top = jnp.max(top, axis=1, keepdims=True)
            weights = [jnp.exp2((piece - top) * EXP2_SCALE) for piece in pieces]
            total = weights[0]
            for piece in weights[1:]:
                total = total + piece
            total = jnp.sum(total, axis=1, keepdims=True)
            rounded = jnp.concatenate([piece.astype(jnp.bfloat16) for piece in weights], axis=1)
            out = dot_nt(rounded, s.values[:, key_at])
            result = jnp.where(lane_head == head, out / total, result)
        return result.astype(jnp.bfloat16)

    def mixed_rows(chunk):
        return aligned(CARRY + chunk * chunk_rows, chunk_rows, CARRY)

    def mix_copies(chunk, at):
        def slot(which):
            return s.others.at[at, pl.ds((which - 1) * width, width)]

        def copy(kind, source, target, device):
            return remote(source, target, s.mix_send.at[kind, chunk], s.mix_recv.at[kind, chunk], {"head": device})

        return (
            copy(0, s.mixed.at[at, :], slot(2), across),
            copy(1, s.mixed.at[at, :], slot(1), sibling),
            copy(2, slot(2), slot(3), sibling),
        )

    carry_at = pl.ds(0, CARRY)
    carry_copies = mix_copies(chunks, carry_at)

    def carry_mask(scores):
        key = lax.broadcasted_iota(jnp.int32, scores.shape, 1)
        row = lax.broadcasted_iota(jnp.int32, scores.shape, 0)
        floor = jnp.where(place < 2, LEAD, 0)
        allowed = (key > row + (LEAD - CARRY)) & (key <= row + (LEAD - CARRY + WINDOW)) & (key >= floor)
        return [jnp.where(allowed, scores, masked_low)]

    s.mixed[carry_at, :] = attend(s.query[LEAD - CARRY : LEAD, :], pl.ds(0, LEAD + WINDOW), carry_mask)
    carry_copies[0].start()
    carry_copies[1].start()

    row = lax.broadcasted_iota(jnp.int32, (chunk_rows, chunk_rows), 0)
    column = lax.broadcasted_iota(jnp.int32, (chunk_rows, chunk_rows), 1)

    def attend_chunk(chunk):
        begin = chunk * chunk_rows
        floor = jnp.where(place == 0, WINDOW - begin, 0)

        def mask(scores):
            pieces = []
            for at in range(0, span, chunk_rows):
                piece = scores[:, at : at + chunk_rows]
                if at == span - chunk_rows:
                    allowed = column <= row
                else:
                    allowed = column >= floor - at
                    if at == 0:
                        allowed = allowed & (column > row)
                pieces.append(jnp.where(allowed, piece, masked_low))
            return pieces

        query = s.query[aligned(LEAD + begin, chunk_rows, chunk_rows), :]
        at = mixed_rows(chunk)
        s.mixed[at, :] = attend(query, aligned(LEAD + begin, span, 128), mask)
        copies = mix_copies(chunk, at)
        copies[0].start()
        copies[1].start()

    def fine_rows(at, start_at):
        merged = dot(s.mixed[at, :], s.cols[:width, :]) + dot(s.others[at, :], s.cols[width:, :])
        value = (s.start[start_at, :].astype(jnp.float32) + merged).astype(jnp.bfloat16).astype(jnp.float32)
        for block in range(lanes):
            s.stream[block, at, :] = value[:, block * 128 : block * 128 + 128]

    peers = (me, sibling, across)
    buffers = (s.send_a, s.recv_a, s.send_b, s.recv_b, s.final)
    short_sum = HeadSum(0, peers, s.part, s.short, buffers, s.sum_send, s.sum_recv)

    def short_rows(chunk):
        return aligned(chunk * group, group, group)

    def relay_chunk(chunk):
        @pl.when(chunk == 0)
        def _():
            carry_copies[0].wait_recv()
            carry_copies[2].start()

        copies = mix_copies(chunk, mixed_rows(chunk))
        copies[0].wait_recv()
        copies[2].start()

    def finish_chunk(chunk):
        @pl.when(chunk == 0)
        def _():
            for copy in column_copies:
                copy.wait_recv()
            loads["cols"].wait()
            loads["ws"].wait()
            carry_copies[1].wait_recv()
            carry_copies[2].wait_recv()
            fine_rows(carry_at, pl.ds(LEAD - CARRY, CARRY))

            @pl.when(place == 0)
            def _():
                s.stream[:, 0:CARRY, :] = jnp.zeros((lanes, CARRY, 128), jnp.float32)

        at = mixed_rows(chunk)
        copies = mix_copies(chunk, at)
        copies[1].wait_recv()
        copies[2].wait_recv()
        fine_rows(at, aligned(LEAD + chunk * chunk_rows, chunk_rows, chunk_rows))
        total = jnp.zeros((group, full), jnp.float32)
        for offset in range(SHORTEN):
            begin = CARRY - (SHORTEN - 1) + offset + chunk * chunk_rows
            member = jnp.concatenate(
                [s.stream[block, pl.ds(begin, group, stride=SHORTEN), :] for block in range(lanes)], axis=1
            )
            total = total + dot(member.astype(jnp.bfloat16), s.ws[offset])
        s.part[short_rows(chunk), :] = total
        short_sum.begin(chunk, short_rows(chunk))

    lane_f = lax.broadcasted_iota(jnp.int32, (rows, 128), 1) % HEAD_DIM
    period_f = periods(lane_f % HALF)
    angle_f = phase(place * rows + lax.broadcasted_iota(jnp.int32, (rows, 128), 0), period_f)
    cos_f = jnp.cos(angle_f)
    sin_f = jnp.where(lane_f < HALF, -jnp.sin(angle_f), jnp.sin(angle_f))
    for block in range(lanes):
        s.coarse_cos[:, block * 128 : block * 128 + 128] = cos_f
        s.coarse_sin[:, block * 128 : block * 128 + 128] = sin_f

    def pair_rows(chunk, source):
        return aligned((chunk * places + source) * group, group, group)

    def pair_copy(chunk, target):
        at = pair_rows(chunk, place)
        return remote(
            s.pair_out.at[target % 2, short_rows(chunk), :], s.pairs.at[at, :],
            s.pair_send.at[target, chunk], s.pair_recv.at[place, chunk], {"seq": target},
        )

    def pair_arrival(chunk, source):
        at = pair_rows(chunk, source)
        return remote(
            s.pairs.at[at, :], s.pairs.at[at, :], s.pair_send.at[source, chunk], s.pair_recv.at[source, chunk],
            {"seq": cross},
        )

    def query_copy(chunk):
        at = short_rows(chunk)
        return remote(
            s.query_out.at[1 - side, at, :], s.queries.at[aligned(side * rows + chunk * group, group, group), :],
            s.query_send.at[chunk], s.query_recv.at[chunk], {"seq": cross},
        )

    def for_targets(action):
        def one(index, state):
            target = places - 1 - index

            @pl.when(target != place)
            def _():
                action(target)

            return state

        lax.fori_loop(0, places - 2 * level, one, 0)

    def project_chunk(chunk):
        @pl.when(chunk == 0)
        def _():
            for name in ("cq", "ck", "cv"):
                loads[name].wait()

        at = short_rows(chunk)
        short_sum.end(chunk, at)
        coarse_in = normed(s.short[at, :].astype(jnp.float32), coarse_gain[...])
        cosine, sine = s.coarse_cos[at, :], s.coarse_sin[at, :]
        is_low = lax.broadcasted_iota(jnp.int32, (group, width), 1) % HEAD_DIM < HALF

        def rotated(values):
            other = jnp.where(is_low, pltpu.roll(values, width - HALF, 1), pltpu.roll(values, HALF, 1))
            return (values * cosine + other * sine).astype(jnp.bfloat16)

        key = rotated(dot(coarse_in, s.ck[...]))
        value = dot(coarse_in, s.cv[...]).astype(jnp.bfloat16)
        for half in range(2):
            s.pair_out[half, at, :pair] = key[:, half * pair : half * pair + pair]
            s.pair_out[half, at, pair:] = value[:, half * pair : half * pair + pair]
        for_targets(lambda target: pair_copy(chunk, target).start())
        query = rotated(dot(coarse_in, s.cq[...]))
        for half in range(2):
            s.query_out[half, at, :] = query[:, half * pair : half * pair + pair]
        query_copy(chunk).start()
        s.pairs[pair_rows(chunk, place), :] = s.pair_out[side, at, :]
        s.queries[aligned(side * rows + chunk * group, group, group), :] = s.query_out[side, at, :]

    def one_step(step, state):
        def staged(lag, action):
            chunk = step - lag

            @pl.when((chunk >= 0) & (chunk < chunks))
            def _():
                action(chunk)

        staged(0, attend_chunk)
        staged(PROJECT, project_chunk)
        staged(TOTAL, lambda chunk: short_sum.total(chunk, short_rows(chunk)))
        staged(MIDDLE, lambda chunk: short_sum.middle(chunk, short_rows(chunk)))
        staged(FINISH, finish_chunk)
        staged(RELAY, relay_chunk)
        return state

    lax.fori_loop(0, chunks + PROJECT, one_step, 0)

    def wait_chunk(chunk):
        def one(source, state):
            @pl.when(source != place)
            def _():
                pair_arrival(chunk, source).wait_recv()

            return state

        lax.fori_loop(0, 2 * level + 2, one, 0)

    def wait_queries(chunk, state):
        query_copy(chunk).wait_recv()
        return state

    lax.fori_loop(0, chunks, wait_queries, 0)

    s.top[...] = jnp.full(s.top.shape, masked_low, jnp.float32)
    s.norm[...] = jnp.zeros(s.norm.shape, jnp.float32)
    s.acc[...] = jnp.zeros(s.acc.shape, jnp.float32)
    per_chunk = places * group
    pair_lane = lax.broadcasted_iota(jnp.int32, (2 * rows, pair), 1) // HEAD_DIM
    queries = s.queries[...]

    def key_step(step, state):
        if per_chunk <= STEP_KEYS:
            for inner in range(STEP_KEYS // per_chunk):
                wait_chunk(step * (STEP_KEYS // per_chunk) + inner)
        else:
            ratio = per_chunk // STEP_KEYS

            @pl.when(step % ratio == 0)
            def _():
                wait_chunk(step // ratio)

        block = s.pairs[aligned(step * STEP_KEYS, STEP_KEYS, STEP_KEYS), :]
        keys, values = block[:, :pair], block[:, pair:]
        index = step * STEP_KEYS + lax.broadcasted_iota(jnp.int32, (1, STEP_KEYS), 1)
        inside = index % per_chunk
        key_at = (inside // group) * rows + (index // per_chunk) * group + inside % group
        query_at = 2 * level * rows + lax.broadcasted_iota(jnp.int32, (2 * rows, 1), 0)
        allowed = key_at <= query_at
        for head in range(pair // HEAD_DIM):
            masked_q = jnp.where(pair_lane == head, queries, jnp.zeros_like(queries))
            scores = jnp.where(allowed, dot_nt(masked_q, keys), masked_low)
            fresh = jnp.maximum(s.top[head], jnp.max(scores, axis=1, keepdims=True))
            factor = jnp.exp2((s.top[head] - fresh) * EXP2_SCALE)
            weights = jnp.exp2((scores - fresh) * EXP2_SCALE)
            s.norm[head] = s.norm[head] * factor + jnp.sum(weights, axis=1, keepdims=True)
            s.acc[head] = s.acc[head] * factor + dot(weights.astype(jnp.bfloat16), values)
            s.top[head] = fresh
        return state

    lax.fori_loop(0, places * rows // STEP_KEYS, key_step, 0)

    def turn_copy():
        return remote(
            s.turn, s.heads_in.at[:, aligned(side * pair, pair, pair)],
            s.turn_send.at[0], s.turn_recv.at[0], {"seq": cross},
        )

    def mixed_of(at):
        result = jnp.zeros((rows, pair), jnp.float32)
        for head in range(pair // HEAD_DIM):
            result = jnp.where(pair_lane[:rows] == head, s.acc[head, at, :] / s.norm[head, at, :], result)
        return result.astype(jnp.bfloat16)

    s.turn[...] = mixed_of(aligned((1 - side) * rows, rows, rows))
    turn_copy().start()
    s.heads_in[:, aligned(side * pair, pair, pair)] = mixed_of(aligned(side * rows, rows, rows))
    loads["co"].wait()
    turn_copy().wait_recv()

    out_sum = HeadSum(1, peers, s.part, s.summed, buffers, s.sum_send, s.sum_recv)
    ffn_sum = HeadSum(2, peers, s.part_b, s.second, buffers, s.sum_send, s.sum_recv)
    size = rows // PIECES
    at = [pl.ds(piece * size, size) for piece in range(PIECES)]

    for piece in range(PIECES):
        s.part[at[piece], :] = dot(s.heads_in[at[piece], :], s.co[...])
        out_sum.begin(piece, at[piece])
    for name in ("up", "down", "lift"):
        loads[name].wait()
    for piece in range(PIECES):
        out_sum.middle(piece, at[piece])

    def feed(piece):
        out_sum.end(piece, at[piece])
        value = s.short[at[piece], :].astype(jnp.float32) + s.summed[at[piece], :].astype(jnp.float32)
        s.first[at[piece], :] = value
        inner = jax.nn.gelu(dot(normed(value, ffn_gain[...]), s.up[...])).astype(jnp.bfloat16)
        s.part_b[at[piece], :] = dot(inner, s.down[...])
        ffn_sum.begin(piece, at[piece])

    def raise_rows(piece):
        ffn_sum.end(piece, at[piece])
        for member in range(SHORTEN):
            lifted = dot(s.second[at[piece], :], s.lift[:, member * width : (member + 1) * width])
            for block in range(lanes):
                s.spread[block, pl.ds(SHORTEN * size * piece + member, size, stride=SHORTEN), :] = lifted[
                    :, block * 128 : block * 128 + 128
                ]
        for block in range(lanes):
            to = slice(SHORTEN * size * piece, SHORTEN * size * (piece + 1))
            base_at = slice(CARRY + SHORTEN * size * piece, CARRY + SHORTEN * size * (piece + 1))
            out_ref[to, block * 128 : block * 128 + 128] = (
                s.stream[block, base_at, :] + s.spread[block, to, :]
            ).astype(jnp.bfloat16)

    for step in range(PIECES + 4):
        if step < PIECES:
            out_sum.total(step, at[step])
        if 0 <= step - 1 < PIECES:
            feed(step - 1)
        if 0 <= step - 2 < PIECES:
            ffn_sum.middle(step - 2, at[step - 2])
        if 0 <= step - 3 < PIECES:
            ffn_sum.total(step - 3, at[step - 3], s.first)
        if 0 <= step - 4 < PIECES:
            raise_rows(step - 4)

    for steps in (1, 2):
        @pl.when(place + steps < places)
        def _():
            id_copy(steps).wait_send()

    for copy in column_copies:
        copy.wait_send()
    for copy in carry_copies:
        copy.wait_send()

    def drain(chunk, state):
        for copy in mix_copies(chunk, mixed_rows(chunk)):
            copy.wait_send()
        short_sum.drain(chunk, short_rows(chunk))
        for_targets(lambda target: pair_copy(chunk, target).wait_send())
        query_copy(chunk).wait_send()
        return state

    lax.fori_loop(0, chunks, drain, 0)
    turn_copy().wait_send()
    for piece in range(PIECES):
        out_sum.drain(piece, at[piece])
        ffn_sum.drain(piece, at[piece])


def local(
    token_ids,
    embedding,
    fine_norm,
    fine_query,
    fine_key,
    fine_value,
    fine_output,
    shorten_weight,
    coarse_norm,
    coarse_query,
    coarse_key,
    coarse_value,
    coarse_output,
    ffn_norm,
    ffn_up,
    ffn_down,
    upsample_weight,
):
    count = token_ids.shape[0]
    width = fine_query.shape[1]
    chunk_rows = min(128, count)
    chunks = count // chunk_rows
    scratch = scratch_list(count, width, chunks, lax.axis_size("seq"))
    names = [name for name, _ in scratch]

    def kernel(*refs):
        block_kernel(names, chunk_rows, *refs)

    return pl.pallas_call(
        kernel,
        out_shape=jax.ShapeDtypeStruct((count, width), jnp.bfloat16),
        in_specs=[VMEM_SPEC] * 4 + [ANY_SPEC] * 13,
        out_specs=VMEM_SPEC,
        scratch_shapes=[shape for _, shape in scratch],
        compiler_params=pltpu.CompilerParams(
            collective_id=1, has_side_effects=True, vmem_limit_bytes=60 * 2**20
        ),
        name="block_kernel",
    )(
        token_ids.reshape(1, count),
        fine_norm.reshape(1, D),
        coarse_norm.reshape(1, D),
        ffn_norm.reshape(1, D),
        embedding,
        fine_query,
        fine_key,
        fine_value,
        fine_output,
        shorten_weight,
        coarse_query,
        coarse_key,
        coarse_value,
        coarse_output,
        ffn_up,
        ffn_down,
        upsample_weight.reshape(D, SHORTEN * width),
    )


def solution(mesh):
    return jax.shard_map(
        local,
        mesh=mesh,
        in_specs=(
            P("seq"),
            P(),
            P(),
            P(None, "head"),
            P(None, "head"),
            P(None, "head"),
            P("head", None),
            P(None, "head", None),
            P(),
            P(None, "head"),
            P(None, "head"),
            P(None, "head"),
            P("head", None),
            P(),
            P(None, "head"),
            P("head", None),
            P(None, None, "head"),
        ),
        out_specs=P("seq", "head"),
        check_vma=False,
    )
```

profile of v0, /device:TPU:1, one launch (start us, length us, event | category | flops | bytes accessed | tf_op | source)
XLA Modules:
  0.0 95.2 jit_solution(1847251518333665130)
XLA Ops:
  0.0 3.4 %copy.18 = bf16[128,8,4,256]{3,1,2,0:T(8,128)(2,1)} copy(bf16[128,8,4,256]{3,2,1,0:T(4,128)(2,1)} %bitcast.7) | data formatting | bytes 4194304
  3.4 89.9 %block_kernel.1 = bf16[1024,256]{1,0:T(8,128)(2,1)} custom-call(s32[1,1024]{1,0:T(1,128)} %bitcast.8, f32[1,1024]{1,0:T(1,128)} %bitcast.9, f32[1,1024]{1,0:T(1,128)} %bitcast.10, f32[1,1024]{1,0:T(1,128)} %bitcast.11, bf16[256,1024]{1,0:T(8,128)(2,1)} %refs_4_.1, bf16[1024,256]{1,0:T(8,128)(2,1)} %refs_5_.1, bf16[1024,256]{1,0:T(8,128)(2,1)} %refs_6_.1, ...), custom_call_target="tpu_custom_call" | custom-call | tf_op jit(solution)/shard_map/block_kernel/pallas_call | solution.py:768
  93.3 1.9 %copy.20 = bf16[1024,256]{1,0:T(8,128)(2,1)} copy(bf16[1024,256]{1,0:T(8,128)(2,1)} %block_kernel.1) | data formatting | bytes 1048576
where the time goes:
time: 95.4 us; the launch traced here: 95.2 us
  Pallas kernels  89.9 us (94%)
  local copies, waits for them, and re-layouts  5.31 us (6%)
    pallas_call x1, Pallas kernels, local(): pl.pallas_call(kernel, out_shape=jax.ShapeDtypeStruct((count, width), jnp...  89.9 us
    unnamed x2, local copies, waits for them, and re-layouts  5.31 us

commit v1 on v0

--- a/solution.py
+++ b/solution.py
@@ -22,7 +22,7 @@
 VMEM_SPEC = pl.BlockSpec(memory_space=pltpu.VMEM)
 ANY_SPEC = pl.BlockSpec(memory_space=pl.ANY)
 
-RELAY, FINISH, MIDDLE, TOTAL, PROJECT, FORWARD = (2, 3, 4, 5, 6, 8)
+RELAY, FINISH, MIDDLE, TOTAL, PROJECT = (2, 3, 4, 6, 7)
 STEP_KEYS = 512
 PIECES = 2
 
@@ -150,9 +150,9 @@
         ("tabs", pltpu.VMEM((6, 256, width), low)),
         ("cos_t", pltpu.VMEM((HALF, frame), wide)),
         ("sin_t", pltpu.VMEM((HALF, frame), wide)),
-        ("keys", pltpu.VMEM((width, frame), low)),
+        ("keys", pltpu.VMEM((frame, width), low)),
         ("values", pltpu.VMEM((width, frame), low)),
-        ("query", pltpu.VMEM((LEAD + count, width), low)),
+        ("query", pltpu.VMEM((width, LEAD + count), low)),
         ("start", pltpu.VMEM((LEAD + count, width), low)),
         ("mixed", pltpu.VMEM((CARRY + count, width), low)),
         ("others", pltpu.VMEM((CARRY + count, 3 * width), low)),
@@ -182,9 +182,9 @@
         ("pair_recv", dma((places, chunks))),
         ("query_send", dma((chunks,))),
         ("query_recv", dma((chunks,))),
-        ("top", pltpu.VMEM((2, 2 * rows, 1), wide)),
-        ("norm", pltpu.VMEM((2, 2 * rows, 1), wide)),
-        ("acc", pltpu.VMEM((2, 2 * rows, width // 2), wide)),
+        ("top", pltpu.VMEM((2, 1, 2 * rows), wide)),
+        ("norm", pltpu.VMEM((2, 1, 2 * rows), wide)),
+        ("acc", pltpu.VMEM((width // 2, 2 * rows), wide)),
         ("turn", pltpu.VMEM((rows, width // 2), low)),
         ("heads_in", pltpu.VMEM((rows, width), low)),
         ("turn_send", dma((1,))),
@@ -328,11 +328,6 @@
     s.tabs[3], s.tabs[4] = split(dot(level_in, s.fq[...]).T)
     s.tabs[5] = s.emb[:, own_columns]
 
-    for steps in (1, 2):
-        @pl.when(place >= steps)
-        def _():
-            id_copy(steps).wait_recv()
-
     def turned(joined, at):
         cosine, sine = s.cos_t[:, at], s.sin_t[:, at]
         pieces = []
@@ -342,52 +337,54 @@
             pieces += [low * cosine - high * sine, high * cosine + low * sine]
         return jnp.concatenate(pieces, axis=0)
 
-    def token_rows(begin, size, queries):
+    def hot_rows(at, size):
+        levels_at = lax.broadcasted_iota(jnp.int32, (256, size), 0)
+        return jnp.where(levels_at == s.ids[:, at], 1.0, 0.0).astype(jnp.bfloat16)
+
+    def key_rows(begin, size):
         at = aligned(begin, size, 128)
-        levels_at = lax.broadcasted_iota(jnp.int32, (256, size), 0)
-        hot = jnp.where(levels_at == s.ids[:, at], 1.0, 0.0).astype(jnp.bfloat16)
-        s.keys[:, at] = turned(dot(s.tabs[0], hot) + dot(s.tabs[1], hot), at).astype(jnp.bfloat16)
+        hot = hot_rows(at, size)
+        s.keys[at, :] = turned(dot(s.tabs[0], hot) + dot(s.tabs[1], hot), at).T.astype(jnp.bfloat16)
         s.values[:, at] = dot(s.tabs[2], hot).astype(jnp.bfloat16)
-        if queries:
-            to = aligned(begin - WINDOW, size, 128)
-            turned_q = turned(dot(s.tabs[3], hot) + dot(s.tabs[4], hot), at)
-            s.query[to, :] = turned_q.T.astype(jnp.bfloat16)
-            s.start[to, :] = dot_tn(hot, s.tabs[5]).astype(jnp.bfloat16)
-
-    early = 256
-    late = (LEAD + count) // 3
-
-    def early_rows(index, state):
-        token_rows(index * early, early, False)
+
+    def query_rows(begin, size):
+        at = aligned(begin, size, 128)
+        to = aligned(begin - WINDOW, size, 128)
+        hot = hot_rows(at, size)
+        s.query[:, to] = turned(dot(s.tabs[3], hot) + dot(s.tabs[4], hot), at).astype(jnp.bfloat16)
+        s.start[to, :] = dot_tn(hot, s.tabs[5]).astype(jnp.bfloat16)
+
+    own_block = min(512, count)
+
+    def own_rows(index, state):
+        key_rows(LEAD + WINDOW + index * own_block, own_block)
+        query_rows(LEAD + WINDOW + index * own_block, own_block)
         return state
 
-    def late_rows(index, state):
-        token_rows(WINDOW + index * late, late, True)
+    def prior_rows(index, state):
+        key_rows(index * 384, 384)
         return state
 
-    lax.fori_loop(0, WINDOW // early, early_rows, 0)
-    lax.fori_loop(0, 3, late_rows, 0)
-
-    def attend(query, key_at, mask):
-        size = query.shape[0]
-        lane_head = lax.broadcasted_iota(jnp.int32, (size, width), 1) // HEAD_DIM
-        result = jnp.zeros((size, width), jnp.float32)
-        for head in range(heads):
-            masked_q = jnp.where(lane_head == head, query, jnp.zeros_like(query))
-            pieces = mask(dot(masked_q, s.keys[:, key_at]))
-            top = pieces[0]
-            for piece in pieces[1:]:
-                top = jnp.maximum(top, piece)
-            top = jnp.max(top, axis=1, keepdims=True)
-            weights = [jnp.exp2((piece - top) * EXP2_SCALE) for piece in pieces]
-            total = weights[0]
-            for piece in weights[1:]:
-                total = total + piece
-            total = jnp.sum(total, axis=1, keepdims=True)
-            rounded = jnp.concatenate([piece.astype(jnp.bfloat16) for piece in weights], axis=1)
-            out = dot_nt(rounded, s.values[:, key_at])
-            result = jnp.where(lane_head == head, out / total, result)
-        return result.astype(jnp.bfloat16)
+    lax.fori_loop(0, count // own_block, own_rows, 0)
+    for steps in (1, 2):
+        @pl.when(place >= steps)
+        def _():
+            id_copy(steps).wait_recv()
+
+    lax.fori_loop(0, (LEAD + WINDOW) // 384, prior_rows, 0)
+    query_rows(WINDOW, LEAD)
+
+    def weigh(scores):
+        top = scores[0]
+        for piece in scores[1:]:
+            top = jnp.maximum(top, piece)
+        top = jnp.max(top, axis=0, keepdims=True)
+        weights = [jnp.exp2((piece - top) * EXP2_SCALE) for piece in scores]
+        total = weights[0]
+        for piece in weights[1:]:
+            total = total + piece
+        total = jnp.sum(total, axis=0, keepdims=True)
+        return jnp.concatenate([piece.astype(jnp.bfloat16) for piece in weights], axis=0), total
 
     def mixed_rows(chunk):
         return aligned(CARRY + chunk * chunk_rows, chunk_rows, CARRY)
@@ -408,40 +405,52 @@
     carry_at = pl.ds(0, CARRY)
     carry_copies = mix_copies(chunks, carry_at)
 
-    def carry_mask(scores):
-        key = lax.broadcasted_iota(jnp.int32, scores.shape, 1)
-        row = lax.broadcasted_iota(jnp.int32, scores.shape, 0)
-        floor = jnp.where(place < 2, LEAD, 0)
-        allowed = (key > row + (LEAD - CARRY)) & (key <= row + (LEAD - CARRY + WINDOW)) & (key >= floor)
-        return [jnp.where(allowed, scores, masked_low)]
-
-    s.mixed[carry_at, :] = attend(s.query[LEAD - CARRY : LEAD, :], pl.ds(0, LEAD + WINDOW), carry_mask)
+    lane_slot = lax.broadcasted_iota(jnp.int32, (HEAD_DIM, LEAD), 1) // 32
+    packed = []
+    for head in range(heads):
+        rolled = pltpu.roll(s.query[head * HEAD_DIM : (head + 1) * HEAD_DIM, :LEAD].astype(jnp.float32), (32 * head + 32) % LEAD, 1)
+        packed.append(jnp.where(lane_slot == head, rolled, 0.0))
+    packed = jnp.concatenate(packed, axis=0).astype(jnp.bfloat16)
+    scores = dot(s.keys[: LEAD + WINDOW, :], packed)
+    key = lax.broadcasted_iota(jnp.int32, scores.shape, 0)
+    last = lax.broadcasted_iota(jnp.int32, scores.shape, 1) % 32 + (LEAD + WINDOW - 32)
+    floor = jnp.where(place < 2, LEAD, 0)
+    allowed = (key > last - WINDOW) & (key <= last) & (key >= floor)
+    weights, total = weigh([jnp.where(allowed, scores, masked_low)])
+    out = dot(s.values[:, : LEAD + WINDOW], weights) / total
+    unpacked = [
+        pltpu.roll(out[head * HEAD_DIM : (head + 1) * HEAD_DIM, :], (LEAD - 32 * head) % LEAD, 1) for head in range(heads)
+    ]
+    s.mixed[carry_at, :] = jnp.concatenate(unpacked, axis=0).T[32 - CARRY : 32, :].astype(jnp.bfloat16)
     carry_copies[0].start()
     carry_copies[1].start()
 
     row = lax.broadcasted_iota(jnp.int32, (chunk_rows, chunk_rows), 0)
     column = lax.broadcasted_iota(jnp.int32, (chunk_rows, chunk_rows), 1)
+    row_head = lax.broadcasted_iota(jnp.int32, (width, chunk_rows), 0) // HEAD_DIM
 
     def attend_chunk(chunk):
         begin = chunk * chunk_rows
         floor = jnp.where(place == 0, WINDOW - begin, 0)
-
-        def mask(scores):
+        key_at = aligned(LEAD + begin, span, 128)
+        query = s.query[:, aligned(LEAD + begin, chunk_rows, chunk_rows)]
+        outs = []
+        for head in range(heads):
+            scores = dot(s.keys[key_at, :], jnp.where(row_head == head, query, jnp.zeros_like(query)))
             pieces = []
             for at in range(0, span, chunk_rows):
-                piece = scores[:, at : at + chunk_rows]
+                piece = scores[at : at + chunk_rows, :]
                 if at == span - chunk_rows:
-                    allowed = column <= row
+                    allowed = row <= column
                 else:
-                    allowed = column >= floor - at
+                    allowed = row >= floor - at
                     if at == 0:
-                        allowed = allowed & (column > row)
+                        allowed = allowed & (row > column)
                 pieces.append(jnp.where(allowed, piece, masked_low))
-            return pieces
-
-        query = s.query[aligned(LEAD + begin, chunk_rows, chunk_rows), :]
+            weights, total = weigh(pieces)
+            outs.append(dot(s.values[head * HEAD_DIM : (head + 1) * HEAD_DIM, key_at], weights) / total)
         at = mixed_rows(chunk)
-        s.mixed[at, :] = attend(query, aligned(LEAD + begin, span, 128), mask)
+        s.mixed[at, :] = jnp.concatenate(outs, axis=0).T.astype(jnp.bfloat16)
         copies = mix_copies(chunk, at)
         copies[0].start()
         copies[1].start()
@@ -573,23 +582,41 @@
         s.pairs[pair_rows(chunk, place), :] = s.pair_out[side, at, :]
         s.queries[aligned(side * rows + chunk * group, group, group), :] = s.query_out[side, at, :]
 
+    stages = (
+        (PROJECT, project_chunk),
+        (TOTAL, lambda chunk: short_sum.total(chunk, short_rows(chunk))),
+        (MIDDLE, lambda chunk: short_sum.middle(chunk, short_rows(chunk))),
+        (FINISH, finish_chunk),
+        (RELAY, relay_chunk),
+    )
+
     def one_step(step, state):
-        def staged(lag, action):
-            chunk = step - lag
-
-            @pl.when((chunk >= 0) & (chunk < chunks))
+        attend_chunk(step)
+        for lag, action in stages:
+            @pl.when(step >= lag)
             def _():
-                action(chunk)
-
-        staged(0, attend_chunk)
-        staged(PROJECT, project_chunk)
-        staged(TOTAL, lambda chunk: short_sum.total(chunk, short_rows(chunk)))
-        staged(MIDDLE, lambda chunk: short_sum.middle(chunk, short_rows(chunk)))
-        staged(FINISH, finish_chunk)
-        staged(RELAY, relay_chunk)
+                action(step - lag)
+
         return state
 
-    lax.fori_loop(0, chunks + PROJECT, one_step, 0)
+    lax.fori_loop(0, chunks, one_step, 0)
+
+    left = {action: max(0, chunks - lag) for lag, action in stages}
+    project, total_up, middle_up, finish, relay = (action for _, action in stages)
+
+    def rest(action, upto):
+        for chunk in range(left[action], min(upto, chunks)):
+            action(chunk)
+        left[action] = max(left[action], min(upto, chunks))
+
+    for action, upto in (
+        (total_up, chunks - 5), (project, chunks - 6), (relay, chunks - 1), (total_up, chunks - 4), (project, chunks - 5),
+        (finish, chunks - 2), (project, chunks - 4), (middle_up, chunks - 3), (relay, chunks), (finish, chunks - 1),
+        (middle_up, chunks - 2), (finish, chunks), (middle_up, chunks - 1), (total_up, chunks - 3), (middle_up, chunks),
+        (project, chunks - 3), (total_up, chunks - 2), (project, chunks - 2), (total_up, chunks - 1), (total_up, chunks),
+        (project, chunks - 1), (project, chunks),
+    ):
+        rest(action, upto)
 
     def wait_chunk(chunk):
         def one(source, state):
@@ -627,19 +654,21 @@
 
         block = s.pairs[aligned(step * STEP_KEYS, STEP_KEYS, STEP_KEYS), :]
         keys, values = block[:, :pair], block[:, pair:]
-        index = step * STEP_KEYS + lax.broadcasted_iota(jnp.int32, (1, STEP_KEYS), 1)
+        index = step * STEP_KEYS + lax.broadcasted_iota(jnp.int32, (STEP_KEYS, 1), 0)
         inside = index % per_chunk
         key_at = (inside // group) * rows + (index // per_chunk) * group + inside % group
-        query_at = 2 * level * rows + lax.broadcasted_iota(jnp.int32, (2 * rows, 1), 0)
+        query_at = 2 * level * rows + lax.broadcasted_iota(jnp.int32, (1, 2 * rows), 1)
         allowed = key_at <= query_at
+        values_t = values.astype(jnp.float32).T.astype(jnp.bfloat16)
         for head in range(pair // HEAD_DIM):
             masked_q = jnp.where(pair_lane == head, queries, jnp.zeros_like(queries))
-            scores = jnp.where(allowed, dot_nt(masked_q, keys), masked_low)
-            fresh = jnp.maximum(s.top[head], jnp.max(scores, axis=1, keepdims=True))
+            scores = jnp.where(allowed, dot_nt(keys, masked_q), masked_low)
+            fresh = jnp.maximum(s.top[head], jnp.max(scores, axis=0, keepdims=True))
             factor = jnp.exp2((s.top[head] - fresh) * EXP2_SCALE)
             weights = jnp.exp2((scores - fresh) * EXP2_SCALE)
-            s.norm[head] = s.norm[head] * factor + jnp.sum(weights, axis=1, keepdims=True)
-            s.acc[head] = s.acc[head] * factor + dot(weights.astype(jnp.bfloat16), values)
+            s.norm[head] = s.norm[head] * factor + jnp.sum(weights, axis=0, keepdims=True)
+            of = slice(head * HEAD_DIM, (head + 1) * HEAD_DIM)
+            s.acc[of, :] = s.acc[of, :] * factor + dot(values_t[of, :], weights.astype(jnp.bfloat16))
             s.top[head] = fresh
         return state
 
@@ -652,10 +681,10 @@
         )
 
     def mixed_of(at):
-        result = jnp.zeros((rows, pair), jnp.float32)
-        for head in range(pair // HEAD_DIM):
-            result = jnp.where(pair_lane[:rows] == head, s.acc[head, at, :] / s.norm[head, at, :], result)
-        return result.astype(jnp.bfloat16)
+        shares = [
+            s.acc[head * HEAD_DIM : (head + 1) * HEAD_DIM, at] / s.norm[head, :, at] for head in range(pair // HEAD_DIM)
+        ]
+        return jnp.concatenate(shares, axis=0).T.astype(jnp.bfloat16)
 
     s.turn[...] = mixed_of(aligned((1 - side) * rows, rows, rows))
     turn_copy().start()
@@ -772,7 +801,7 @@
         out_specs=VMEM_SPEC,
         scratch_shapes=[shape for _, shape in scratch],
         compiler_params=pltpu.CompilerParams(
-            collective_id=1, has_side_effects=True, vmem_limit_bytes=60 * 2**20
+            collective_id=1, has_side_effects=True, vmem_limit_bytes=42 * 2**20
         ),
         name="block_kernel",
     )(

time: 95.4 us -> 105 us (1.10)
  local copies, waits for them, and re-layouts: 5.31 us -> 18.1 us
  Pallas kernels: 89.9 us -> 86.7 us
    unnamed x2 -> x34, local copies, waits for them, and re-layouts: 5.31 us -> 18.1 us
    pallas_call x1, Pallas kernels: 89.9 us -> 86.7 us  [local(): pl.pallas_call(kernel, out_shape=jax.ShapeDtypeStruct((count, width), jnp...]
where the time goes in v1:
time: 105 us
  Pallas kernels  86.7 us (83%)
  local copies, waits for them, and re-layouts  18.1 us (17%)
    pallas_call x1, Pallas kernels, local(): pl.pallas_call(kernel, out_shape=jax.ShapeDtypeStruct((count, width), jnp...  86.7 us
    unnamed x34, local copies, waits for them, and re-layouts  18.1 us

profile of v1, /device:TPU:1, one launch (start us, length us, event | category | flops | bytes accessed | tf_op | source)
XLA Modules:
  0.0 104.8 jit_solution(12631303867509596396)
XLA Ops:
  0.0 0.0 copy-start
  0.0 0.0 copy-start.1
  0.0 3.6 %copy.18 = bf16[128,8,4,256]{3,1,2,0:T(8,128)(2,1)} copy(bf16[128,8,4,256]{3,2,1,0:T(4,128)(2,1)} %bitcast.11) | data formatting | bytes 4194304
  3.6 0.0 copy-done
  3.6 0.0 copy-done.1
  3.6 0.0 copy-start.2
  3.6 1.6 %copy-done.2 = bf16[1024,1024]{1,0:T(8,128)(2,1)S(1)} copy-done((bf16[1024,1024]{1,0:T(8,128)(2,1)S(1)}, bf16[1024,1024]{1,0:T(8,128)(2,1)}, u32[]{:S(2)}) %copy-start.2) | copy-done | bytes 2097176
  5.2 0.0 copy-start.3
  5.2 1.0 copy-done.3
  6.2 0.0 copy-start.4
  6.2 1.0 copy-done.4
  7.3 0.0 copy-start.5
  7.3 1.0 copy-done.5
  8.3 0.0 copy-start.6
  8.3 1.0 copy-done.6
  9.4 0.0 copy-start.7
  9.4 1.0 copy-done.7
  10.4 0.0 copy-start.8
  10.4 1.0 copy-done.8
  11.4 0.0 copy-start.9
  11.4 1.0 copy-done.9
  12.5 0.0 copy-start.10
  12.5 1.0 copy-done.10
  13.5 0.0 copy-start.11
  13.5 1.0 copy-done.11
  14.6 0.0 copy-start.12
  14.6 0.7 copy-done.12
  15.3 0.0 copy-start.13
  15.3 0.7 copy-done.13
  15.9 0.0 copy-start.14
  15.9 0.7 copy-done.14
  16.6 0.0 copy-start.15
  16.6 0.7 copy-done.15
  17.3 86.7 %block_kernel.1 = bf16[1024,256]{1,0:T(8,128)(2,1)S(1)} custom-call(s32[1,1024]{1,0:T(1,128)S(1)} %bitcast.6, f32[1,1024]{1,0:T(1,128)S(1)} %bitcast.7, f32[1,1024]{1,0:T(1,128)S(1)} %bitcast.8, f32[1,1024]{1,0:T(1,128)S(1)} %bitcast.9, bf16[256,1024]{1,0:T(8,128)(2,1)S(1)} %copy-done.3, bf16[1024,256]{1,0:T(8,128)(2,1)S(1)} %copy-done.4, ...), custom_call_target="tpu_custom_call" | custom-call | tf_op jit(solution)/shard_map/block_kernel/pallas_call | solution.py:797
  104.0 0.8 copy.20
Async XLA Ops:
  0.0 3.6 %copy-start = (bf16[4,256,1024]{2,1,0:T(8,128)(2,1)S(1)}, bf16[4,256,1024]{2,1,0:T(8,128)(2,1)}, u32[]{:S(2)}) copy-start(bf16[4,256,1024]{2,1,0:T(8,128)(2,1)} %refs_9_.1) | copy-start | bytes 6291460
  0.0 3.6 %copy-start.1 = (bf16[1024,1024]{1,0:T(8,128)(2,1)S(1)}, bf16[1024,1024]{1,0:T(8,128)(2,1)}, u32[]{:S(2)}) copy-start(bf16[1024,1024]{1,0:T(8,128)(2,1)} %refs_14_.1) | copy-start | bytes 6291460
  3.6 1.6 %copy-start.2 = (bf16[1024,1024]{1,0:T(8,128)(2,1)S(1)}, bf16[1024,1024]{1,0:T(8,128)(2,1)}, u32[]{:S(2)}) copy-start(bf16[1024,1024]{1,0:T(8,128)(2,1)} %refs_15_.1) | copy-start | bytes 6291460
  5.2 1.0 copy-start.3
  6.2 1.0 copy-start.4
  7.3 1.0 copy-start.5
  8.3 1.0 copy-start.6
  9.4 1.0 copy-start.7
  10.4 1.0 copy-start.8
  11.4 1.0 copy-start.9
  12.5 1.0 copy-start.10
  13.5 1.0 copy-start.11
  14.6 0.7 copy-start.12
  15.3 0.7 copy-start.13
  15.9 0.7 copy-start.14
  16.6 0.7 copy-start.15

commit v2 on v1

--- a/solution.py
+++ b/solution.py
@@ -20,7 +20,7 @@
 MESH = pl.DeviceIdType.MESH
 EXP2_SCALE = HEAD_DIM ** (-0.5) * math.log2(math.e)
 VMEM_SPEC = pl.BlockSpec(memory_space=pltpu.VMEM)
-ANY_SPEC = pl.BlockSpec(memory_space=pl.ANY)
+HBM_SPEC = pl.BlockSpec(memory_space=pltpu.HBM)
 
 RELAY, FINISH, MIDDLE, TOTAL, PROJECT = (2, 3, 4, 6, 7)
 STEP_KEYS = 512
@@ -141,7 +141,11 @@
         ("up", pltpu.VMEM((full, full), low)),
         ("down", pltpu.VMEM((full, full), low)),
         ("lift", pltpu.VMEM((full, SHORTEN * width), low)),
-        ("load_sem", dma((13,))),
+        ("raw", pltpu.VMEM((width // 128, full, SHORTEN, 128), low)),
+        ("fine_gain", pltpu.VMEM((1, full), wide)),
+        ("coarse_gain", pltpu.VMEM((1, full), wide)),
+        ("ffn_gain", pltpu.VMEM((1, full), wide)),
+        ("load_sem", dma((17 + width // 128,))),
         ("ids", pltpu.VMEM((1, frame), jnp.int32)),
         ("id_send", dma((2,))),
         ("id_recv", dma((2,))),
@@ -198,7 +202,7 @@
 
 
 def block_kernel(names, chunk_rows, *refs):
-    (ids_ref, fine_gain, coarse_gain, ffn_gain, emb_h, fq_h, fk_h, fv_h, fo_h, ws_h,
+    (ids_h, fine_gain_h, coarse_gain_h, ffn_gain_h, emb_h, fq_h, fk_h, fv_h, fo_h, ws_h,
      cq_h, ck_h, cv_h, co_h, up_h, down_h, lift_h, out_ref) = refs[:18]
     s = Names()
     for name, ref in zip(names, refs[18:]):
@@ -238,19 +242,26 @@
     lax.fori_loop(1, places, greet, 0)
 
     own_columns = aligned(me * width, width, width)
+    own_ids = s.ids.at[:, pl.ds(LEAD + WINDOW, count)]
     loads = {
         name: pltpu.make_async_copy(source, target, s.load_sem.at[index])
         for index, (name, source, target) in enumerate((
-            ("emb", emb_h, s.emb), ("fk", fk_h, s.fk), ("fv", fv_h, s.fv), ("fq", fq_h, s.fq),
+            ("ids", ids_h, own_ids), ("emb", emb_h, s.emb), ("fine_gain", fine_gain_h, s.fine_gain),
+            ("fk", fk_h, s.fk), ("fv", fv_h, s.fv), ("fq", fq_h, s.fq),
+            ("coarse_gain", coarse_gain_h, s.coarse_gain), ("ffn_gain", ffn_gain_h, s.ffn_gain),
             ("cols", fo_h.at[:, own_columns], s.cols.at[pl.ds(0, width), :]),
             ("ws", ws_h, s.ws), ("cq", cq_h, s.cq), ("ck", ck_h, s.ck), ("cv", cv_h, s.cv), ("co", co_h, s.co),
-            ("up", up_h, s.up), ("down", down_h, s.down), ("lift", lift_h, s.lift),
+            ("up", up_h, s.up), ("down", down_h, s.down),
+            *((f"lift{b}", lift_h.at[:, :, pl.ds(b * 128, 128)], s.raw.at[b]) for b in range(lanes)),
         ))
     }
-    for load in loads.values():
-        load.start()
-
-    s.ids[:, LEAD + WINDOW :] = ids_ref[...]
+    lift_names = tuple(f"lift{block}" for block in range(lanes))
+
+    def start_loads(*names):
+        for name in names:
+            loads[name].start()
+
+    start_loads("ids", "emb", "fine_gain", "fk", "fv", "fq")
 
     @pl.when(place < 1)
     def _():
@@ -291,10 +302,10 @@
     def id_copy(steps):
         if steps == 1:
             target = s.ids.at[:, pl.ds(LEAD, WINDOW)]
-            source = ids_ref
+            source = ids_h
         else:
             target = s.ids.at[:, pl.ds(0, LEAD)]
-            source = ids_ref.at[:, pl.ds(count - LEAD, LEAD)]
+            source = ids_h.at[:, pl.ds(count - LEAD, LEAD)]
         device = (place + steps) % places
         return remote(source, target, s.id_send.at[steps - 1], s.id_recv.at[steps - 1], {"seq": device})
 
@@ -314,7 +325,8 @@
         copy.start()
 
     loads["emb"].wait()
-    level_in = normed(s.emb[...].astype(jnp.float32), fine_gain[...])
+    loads["fine_gain"].wait()
+    level_in = normed(s.emb[...].astype(jnp.float32), s.fine_gain[...])
 
     def split(values):
         high = values.astype(jnp.bfloat16)
@@ -327,6 +339,8 @@
     loads["fq"].wait()
     s.tabs[3], s.tabs[4] = split(dot(level_in, s.fq[...]).T)
     s.tabs[5] = s.emb[:, own_columns]
+    loads["ids"].wait()
+    start_loads("cols", "ws", "coarse_gain", "ffn_gain", "cq", "ck", "cv")
 
     def turned(joined, at):
         cosine, sine = s.cos_t[:, at], s.sin_t[:, at]
@@ -404,6 +418,8 @@
 
     carry_at = pl.ds(0, CARRY)
     carry_copies = mix_copies(chunks, carry_at)
+
+    start_loads("co", "up", "down", *lift_names)
 
     lane_slot = lax.broadcasted_iota(jnp.int32, (HEAD_DIM, LEAD), 1) // 32
     packed = []
@@ -556,12 +572,12 @@
     def project_chunk(chunk):
         @pl.when(chunk == 0)
         def _():
-            for name in ("cq", "ck", "cv"):
+            for name in ("coarse_gain", "cq", "ck", "cv"):
                 loads[name].wait()
 
         at = short_rows(chunk)
         short_sum.end(chunk, at)
-        coarse_in = normed(s.short[at, :].astype(jnp.float32), coarse_gain[...])
+        coarse_in = normed(s.short[at, :].astype(jnp.float32), s.coarse_gain[...])
         cosine, sine = s.coarse_cos[at, :], s.coarse_sin[at, :]
         is_low = lax.broadcasted_iota(jnp.int32, (group, width), 1) % HEAD_DIM < HALF
 
@@ -627,6 +643,18 @@
             return state
 
         lax.fori_loop(0, 2 * level + 2, one, 0)
+
+    for name in lift_names:
+        loads[name].wait()
+    part_rows = count // SHORTEN
+    for block in range(lanes):
+        for begin in range(0, full, part_rows):
+            flat = s.raw.at[block, pl.ds(begin, part_rows)].reshape(part_rows * SHORTEN, 128)
+            s.spread[block] = flat[...].astype(jnp.float32)
+            for member in range(SHORTEN):
+                s.lift[begin : begin + part_rows, member * width + block * 128 : member * width + block * 128 + 128] = (
+                    s.spread[block, pl.ds(member, part_rows, stride=SHORTEN), :].astype(jnp.bfloat16)
+                )
 
     def wait_queries(chunk, state):
         query_copy(chunk).wait_recv()
@@ -700,7 +728,7 @@
     for piece in range(PIECES):
         s.part[at[piece], :] = dot(s.heads_in[at[piece], :], s.co[...])
         out_sum.begin(piece, at[piece])
-    for name in ("up", "down", "lift"):
+    for name in ("ffn_gain", "up", "down"):
         loads[name].wait()
     for piece in range(PIECES):
         out_sum.middle(piece, at[piece])
@@ -709,7 +737,7 @@
         out_sum.end(piece, at[piece])
         value = s.short[at[piece], :].astype(jnp.float32) + s.summed[at[piece], :].astype(jnp.float32)
         s.first[at[piece], :] = value
-        inner = jax.nn.gelu(dot(normed(value, ffn_gain[...]), s.up[...])).astype(jnp.bfloat16)
+        inner = jax.nn.gelu(dot(normed(value, s.ffn_gain[...]), s.up[...])).astype(jnp.bfloat16)
         s.part_b[at[piece], :] = dot(inner, s.down[...])
         ffn_sum.begin(piece, at[piece])
 
@@ -797,7 +825,7 @@
     return pl.pallas_call(
         kernel,
         out_shape=jax.ShapeDtypeStruct((count, width), jnp.bfloat16),
-        in_specs=[VMEM_SPEC] * 4 + [ANY_SPEC] * 13,
+        in_specs=[HBM_SPEC] * 17,
         out_specs=VMEM_SPEC,
         scratch_shapes=[shape for _, shape in scratch],
         compiler_params=pltpu.CompilerParams(
@@ -805,23 +833,14 @@
         ),
         name="block_kernel",
     )(
-        token_ids.reshape(1, count),
-        fine_norm.reshape(1, D),
-        coarse_norm.reshape(1, D),
-        ffn_norm.reshape(1, D),
-        embedding,
-        fine_query,
-        fine_key,
-        fine_value,
-        fine_output,
-        shorten_weight,
-        coarse_query,
-        coarse_key,
-        coarse_value,
-        coarse_output,
-        ffn_up,
-        ffn_down,
-        upsample_weight.reshape(D, SHORTEN * width),
+        *(
+            pltpu.with_memory_space_constraint(array, pltpu.HBM)
+            for array in (
+                token_ids.reshape(1, count), fine_norm.reshape(1, D), coarse_norm.reshape(1, D), ffn_norm.reshape(1, D),
+                embedding, fine_query, fine_key, fine_value, fine_output, shorten_weight, coarse_query, coarse_key,
+                coarse_value, coarse_output, ffn_up, ffn_down, upsample_weight,
+            )
+        ),
     )
 
 

time: 105 us -> 87.5 us (0.83)
  local copies, waits for them, and re-layouts: 18.1 us -> 0.8 us
    unnamed x34 -> x1, local copies, waits for them, and re-layouts: 18.1 us -> 0.8 us
where the time goes in v2:
time: 87.5 us; the launch traced here: 87.4 us
  Pallas kernels  86.6 us (99%)
    pallas_call x1, Pallas kernels, local(): pl.pallas_call(kernel, out_shape=jax.ShapeDtypeStruct((count, width), jnp...  86.6 us

profile of v2, /device:TPU:1, one launch (start us, length us, event | category | flops | bytes accessed | tf_op | source)
XLA Modules:
  0.0 87.4 jit_solution(17745876433264614251)
XLA Ops:
  0.0 86.6 %block_kernel.1 = bf16[1024,256]{1,0:T(8,128)(2,1)S(1)} custom-call(s32[1,1024]{1,0:T(1,128)} %bitcast.4, f32[1,1024]{1,0:T(1,128)} %bitcast.5, f32[1,1024]{1,0:T(1,128)} %bitcast.6, f32[1,1024]{1,0:T(1,128)} %bitcast.7, bf16[256,1024]{1,0:T(8,128)(2,1)} %refs_4_.1, bf16[1024,256]{1,0:T(8,128)(2,1)} %refs_5_.1, bf16[1024,256]{1,0:T(8,128)(2,1)} %refs_6_.1, ...), custom_call_target="tpu_custom_call" | custom-call | tf_op jit(solution)/shard_map/block_kernel/pallas_call | solution.py:825
  86.6 0.8 copy.19

commit v3 on v2

--- a/solution.py
+++ b/solution.py
@@ -158,6 +158,8 @@
         ("values", pltpu.VMEM((width, frame), low)),
         ("query", pltpu.VMEM((width, LEAD + count), low)),
         ("start", pltpu.VMEM((LEAD + count, width), low)),
+        ("scores", pltpu.VMEM((WINDOW + count // chunks, 4 * (count // chunks)), wide)),
+        ("weights", pltpu.VMEM((WINDOW + count // chunks, 4 * (count // chunks)), low)),
         ("mixed", pltpu.VMEM((CARRY + count, width), low)),
         ("others", pltpu.VMEM((CARRY + count, 3 * width), low)),
         ("mix_send", dma((3, chunks + 1))),
@@ -441,8 +443,13 @@
     carry_copies[0].start()
     carry_copies[1].start()
 
-    row = lax.broadcasted_iota(jnp.int32, (chunk_rows, chunk_rows), 0)
-    column = lax.broadcasted_iota(jnp.int32, (chunk_rows, chunk_rows), 1)
+    part_keys = 3 * chunk_rows if span % (3 * chunk_rows) == 0 else chunk_rows
+    row = lax.broadcasted_iota(jnp.int32, (chunk_rows, heads * chunk_rows), 0)
+    column = lax.broadcasted_iota(jnp.int32, (chunk_rows, heads * chunk_rows), 1) % chunk_rows
+
+    def by_eights(values):
+        return values.reshape(values.shape[0] // 8, 8, values.shape[1])
+
     row_head = lax.broadcasted_iota(jnp.int32, (width, chunk_rows), 0) // HEAD_DIM
 
     def attend_chunk(chunk):
@@ -450,21 +457,37 @@
         floor = jnp.where(place == 0, WINDOW - begin, 0)
         key_at = aligned(LEAD + begin, span, 128)
         query = s.query[:, aligned(LEAD + begin, chunk_rows, chunk_rows)]
-        outs = []
-        for head in range(heads):
-            scores = dot(s.keys[key_at, :], jnp.where(row_head == head, query, jnp.zeros_like(query)))
-            pieces = []
-            for at in range(0, span, chunk_rows):
-                piece = scores[at : at + chunk_rows, :]
+        stacked = jnp.concatenate(
+            [jnp.where(row_head == head, query, jnp.zeros_like(query)) for head in range(heads)], axis=1
+        )
+        top = None
+        for part in range(0, span, part_keys):
+            scores = dot(s.keys[aligned(LEAD + begin + part, part_keys, 128), :], stacked)
+            for at in range(part, part + part_keys, chunk_rows):
+                piece = scores[at - part : at - part + chunk_rows, :]
                 if at == span - chunk_rows:
                     allowed = row <= column
                 else:
                     allowed = row >= floor - at
                     if at == 0:
                         allowed = allowed & (row > column)
-                pieces.append(jnp.where(allowed, piece, masked_low))
-            weights, total = weigh(pieces)
-            outs.append(dot(s.values[head * HEAD_DIM : (head + 1) * HEAD_DIM, key_at], weights) / total)
+                piece = jnp.where(allowed, piece, masked_low)
+                s.scores[at : at + chunk_rows, :] = piece
+                peak = jnp.max(by_eights(piece), axis=0)
+                top = peak if top is None else jnp.maximum(top, peak)
+        top = jnp.max(top, axis=0, keepdims=True)
+        total = jnp.zeros((8, heads * chunk_rows), jnp.float32)
+        for at in range(0, span, chunk_rows):
+            weights = jnp.exp2((s.scores[at : at + chunk_rows, :] - top) * EXP2_SCALE)
+            total = total + jnp.sum(by_eights(weights), axis=0)
+            s.weights[at : at + chunk_rows, :] = weights.astype(jnp.bfloat16)
+        total = jnp.sum(total, axis=0, keepdims=True)
+        outs = []
+        for head in range(heads):
+            of = slice(head * chunk_rows, (head + 1) * chunk_rows)
+            outs.append(
+                dot(s.values[head * HEAD_DIM : (head + 1) * HEAD_DIM, key_at], s.weights[:, of]) / total[:, of]
+            )
         at = mixed_rows(chunk)
         s.mixed[at, :] = jnp.concatenate(outs, axis=0).T.astype(jnp.bfloat16)
         copies = mix_copies(chunk, at)
@@ -717,6 +740,26 @@
     s.turn[...] = mixed_of(aligned((1 - side) * rows, rows, rows))
     turn_copy().start()
     s.heads_in[:, aligned(side * pair, pair, pair)] = mixed_of(aligned(side * rows, rows, rows))
+
+    for steps in (1, 2):
+        @pl.when(place + steps < places)
+        def _():
+            id_copy(steps).wait_send()
+
+    for copy in column_copies:
+        copy.wait_send()
+    for copy in carry_copies:
+        copy.wait_send()
+
+    def drain(chunk, state):
+        for copy in mix_copies(chunk, mixed_rows(chunk)):
+            copy.wait_send()
+        short_sum.drain(chunk, short_rows(chunk))
+        for_targets(lambda target: pair_copy(chunk, target).wait_send())
+        query_copy(chunk).wait_send()
+        return state
+
+    lax.fori_loop(0, chunks, drain, 0)
     loads["co"].wait()
     turn_copy().wait_recv()
 
@@ -768,25 +811,6 @@
         if 0 <= step - 4 < PIECES:
             raise_rows(step - 4)
 
-    for steps in (1, 2):
-        @pl.when(place + steps < places)
-        def _():
-            id_copy(steps).wait_send()
-
-    for copy in column_copies:
-        copy.wait_send()
-    for copy in carry_copies:
-        copy.wait_send()
-
-    def drain(chunk, state):
-        for copy in mix_copies(chunk, mixed_rows(chunk)):
-            copy.wait_send()
-        short_sum.drain(chunk, short_rows(chunk))
-        for_targets(lambda target: pair_copy(chunk, target).wait_send())
-        query_copy(chunk).wait_send()
-        return state
-
-    lax.fori_loop(0, chunks, drain, 0)
     turn_copy().wait_send()
     for piece in range(PIECES):
         out_sum.drain(piece, at[piece])
@@ -829,7 +853,7 @@
         out_specs=VMEM_SPEC,
         scratch_shapes=[shape for _, shape in scratch],
         compiler_params=pltpu.CompilerParams(
-            collective_id=1, has_side_effects=True, vmem_limit_bytes=42 * 2**20
+            collective_id=1, has_side_effects=True, vmem_limit_bytes=46 * 2**20
         ),
         name="block_kernel",
     )(

time: 87.5 us -> 80.1 us (0.915)
  Pallas kernels: 86.6 us -> 79.2 us
    pallas_call x1, Pallas kernels: 86.6 us -> 79.2 us  [local(): pl.pallas_call(kernel, out_shape=jax.ShapeDtypeStruct((count, width), jnp...]
where the time goes in v3:
time: 80.1 us; the launch traced here: 80 us
  Pallas kernels  79.2 us (99%)
    pallas_call x1, Pallas kernels, local(): pl.pallas_call(kernel, out_shape=jax.ShapeDtypeStruct((count, width), jnp...  79.2 us

profile of v3, /device:TPU:1, one launch (start us, length us, event | category | flops | bytes accessed | tf_op | source)
XLA Modules:
  0.0 80.0 jit_solution(9793798501356925426)
XLA Ops:
  0.0 79.2 %block_kernel.1 = bf16[1024,256]{1,0:T(8,128)(2,1)S(1)} custom-call(s32[1,1024]{1,0:T(1,128)} %bitcast.4, f32[1,1024]{1,0:T(1,128)} %bitcast.5, f32[1,1024]{1,0:T(1,128)} %bitcast.6, f32[1,1024]{1,0:T(1,128)} %bitcast.7, bf16[256,1024]{1,0:T(8,128)(2,1)} %refs_4_.1, bf16[1024,256]{1,0:T(8,128)(2,1)} %refs_5_.1, bf16[1024,256]{1,0:T(8,128)(2,1)} %refs_6_.1, ...), custom_call_target="tpu_custom_call" | custom-call | tf_op jit(solution)/shard_map/block_kernel/pallas_call | solution.py:849
  79.2 0.8 copy.19

commit v4 on v3

--- a/solution.py
+++ b/solution.py
@@ -22,9 +22,11 @@
 VMEM_SPEC = pl.BlockSpec(memory_space=pltpu.VMEM)
 HBM_SPEC = pl.BlockSpec(memory_space=pltpu.HBM)
 
-RELAY, FINISH, MIDDLE, TOTAL, PROJECT = (2, 3, 4, 6, 7)
+RELAY, FINISH, MIDDLE, TOTAL, PROJECT = (2, 2, 3, 5, 5)
+FORWARDED = 5
 STEP_KEYS = 512
 PIECES = 2
+SET = 2
 
 
 def dot(left, right):
@@ -186,6 +188,7 @@
         ("queries", pltpu.VMEM((2 * rows, width // 2), low)),
         ("pair_send", dma((places, chunks))),
         ("pair_recv", dma((places, chunks))),
+        ("forward_send", dma((places, chunks))),
         ("query_send", dma((chunks,))),
         ("query_recv", dma((chunks,))),
         ("top", pltpu.VMEM((2, 1, 2 * rows), wide)),
@@ -444,8 +447,19 @@
     carry_copies[1].start()
 
     part_keys = 3 * chunk_rows if span % (3 * chunk_rows) == 0 else chunk_rows
-    row = lax.broadcasted_iota(jnp.int32, (chunk_rows, heads * chunk_rows), 0)
-    column = lax.broadcasted_iota(jnp.int32, (chunk_rows, heads * chunk_rows), 1) % chunk_rows
+    row = lax.broadcasted_iota(jnp.int32, (chunk_rows, chunk_rows), 0)
+    column = lax.broadcasted_iota(jnp.int32, (chunk_rows, chunk_rows), 1)
+
+    def each_head(allowed, piece):
+        return jnp.concatenate(
+            [
+                jnp.where(allowed, piece[:, head * chunk_rows : (head + 1) * chunk_rows], masked_low)
+                for head in range(piece.shape[1] // chunk_rows)
+            ],
+            axis=1,
+        )
+
+    sets = [tuple(range(first, min(first + SET, heads))) for first in range(0, heads, SET)]
 
     def by_eights(values):
         return values.reshape(values.shape[0] // 8, 8, values.shape[1])
@@ -457,37 +471,40 @@
         floor = jnp.where(place == 0, WINDOW - begin, 0)
         key_at = aligned(LEAD + begin, span, 128)
         query = s.query[:, aligned(LEAD + begin, chunk_rows, chunk_rows)]
-        stacked = jnp.concatenate(
-            [jnp.where(row_head == head, query, jnp.zeros_like(query)) for head in range(heads)], axis=1
-        )
-        top = None
-        for part in range(0, span, part_keys):
-            scores = dot(s.keys[aligned(LEAD + begin + part, part_keys, 128), :], stacked)
-            for at in range(part, part + part_keys, chunk_rows):
-                piece = scores[at - part : at - part + chunk_rows, :]
-                if at == span - chunk_rows:
-                    allowed = row <= column
-                else:
-                    allowed = row >= floor - at
-                    if at == 0:
-                        allowed = allowed & (row > column)
-                piece = jnp.where(allowed, piece, masked_low)
-                s.scores[at : at + chunk_rows, :] = piece
-                peak = jnp.max(by_eights(piece), axis=0)
-                top = peak if top is None else jnp.maximum(top, peak)
-        top = jnp.max(top, axis=0, keepdims=True)
-        total = jnp.zeros((8, heads * chunk_rows), jnp.float32)
-        for at in range(0, span, chunk_rows):
-            weights = jnp.exp2((s.scores[at : at + chunk_rows, :] - top) * EXP2_SCALE)
-            total = total + jnp.sum(by_eights(weights), axis=0)
-            s.weights[at : at + chunk_rows, :] = weights.astype(jnp.bfloat16)
-        total = jnp.sum(total, axis=0, keepdims=True)
+        tops, totals = [], []
+        for side_heads in sets:
+            lanes_of = slice(side_heads[0] * chunk_rows, (side_heads[-1] + 1) * chunk_rows)
+            stacked = jnp.concatenate(
+                [jnp.where(row_head == head, query, jnp.zeros_like(query)) for head in side_heads], axis=1
+            )
+            top = None
+            for part in range(0, span, part_keys):
+                scores = dot(s.keys[aligned(LEAD + begin + part, part_keys, 128), :], stacked)
+                for at in range(part, part + part_keys, chunk_rows):
+                    piece = scores[at - part : at - part + chunk_rows, :]
+                    if at == span - chunk_rows:
+                        piece = each_head(row <= column, piece)
+                    else:
+                        piece = piece + jnp.where(at < floor, masked_low, 0.0)
+                        if at == 0:
+                            piece = each_head(row > column, piece)
+                    s.scores[at : at + chunk_rows, lanes_of] = piece
+                    peak = jnp.max(by_eights(piece), axis=0)
+                    top = peak if top is None else jnp.maximum(top, peak)
+            tops.append(jnp.max(top, axis=0, keepdims=True))
         outs = []
-        for head in range(heads):
-            of = slice(head * chunk_rows, (head + 1) * chunk_rows)
-            outs.append(
-                dot(s.values[head * HEAD_DIM : (head + 1) * HEAD_DIM, key_at], s.weights[:, of]) / total[:, of]
-            )
+        for which, side_heads in enumerate(sets):
+            lanes_of = slice(side_heads[0] * chunk_rows, (side_heads[-1] + 1) * chunk_rows)
+            total = jnp.zeros((8, len(side_heads) * chunk_rows), jnp.float32)
+            for at in range(0, span, chunk_rows):
+                weights = jnp.exp2((s.scores[at : at + chunk_rows, lanes_of] - tops[which]) * EXP2_SCALE)
+                total = total + jnp.sum(by_eights(weights), axis=0)
+                s.weights[at : at + chunk_rows, lanes_of] = weights.astype(jnp.bfloat16)
+            total = jnp.sum(total, axis=0, keepdims=True)
+            for index, head in enumerate(side_heads):
+                of = slice(head * chunk_rows, (head + 1) * chunk_rows)
+                share = dot(s.values[head * HEAD_DIM : (head + 1) * HEAD_DIM, key_at], s.weights[:, of])
+                outs.append(share / total[:, index * chunk_rows : (index + 1) * chunk_rows])
         at = mixed_rows(chunk)
         s.mixed[at, :] = jnp.concatenate(outs, axis=0).T.astype(jnp.bfloat16)
         copies = mix_copies(chunk, at)
@@ -580,17 +597,34 @@
             s.query_send.at[chunk], s.query_recv.at[chunk], {"seq": cross},
         )
 
-    def for_targets(action):
+    def for_targets(chunk, action):
         def one(index, state):
             target = places - 1 - index
 
-            @pl.when(target != place)
+            @pl.when((target != place) & ((target // 2 <= level + 2) | (chunk >= FORWARDED)))
             def _():
                 action(target)
 
             return state
 
         lax.fori_loop(0, places - 2 * level, one, 0)
+
+    forwards = jnp.where(level + 1 < levels, jnp.maximum(2 * (level - 1), 0), 0)
+
+    def forward_copy(chunk, source):
+        at = pair_rows(chunk, source)
+        return remote(
+            s.pairs.at[at, :], s.pairs.at[at, :], s.forward_send.at[source, chunk], s.pair_recv.at[source, chunk],
+            {"seq": (place + 2) % places},
+        )
+
+    def forward_chunk(chunk):
+        def one(source, state):
+            pair_arrival(chunk, source).wait_recv()
+            forward_copy(chunk, source).start()
+            return state
+
+        lax.fori_loop(0, forwards, one, 0)
 
     def project_chunk(chunk):
         @pl.when(chunk == 0)
@@ -613,7 +647,7 @@
         for half in range(2):
             s.pair_out[half, at, :pair] = key[:, half * pair : half * pair + pair]
             s.pair_out[half, at, pair:] = value[:, half * pair : half * pair + pair]
-        for_targets(lambda target: pair_copy(chunk, target).start())
+        for_targets(chunk, lambda target: pair_copy(chunk, target).start())
         query = rotated(dot(coarse_in, s.cq[...]))
         for half in range(2):
             s.query_out[half, at, :] = query[:, half * pair : half * pair + pair]
@@ -621,45 +655,49 @@
         s.pairs[pair_rows(chunk, place), :] = s.pair_out[side, at, :]
         s.queries[aligned(side * rows + chunk * group, group, group), :] = s.query_out[side, at, :]
 
-    stages = (
-        (PROJECT, project_chunk),
-        (TOTAL, lambda chunk: short_sum.total(chunk, short_rows(chunk))),
-        (MIDDLE, lambda chunk: short_sum.middle(chunk, short_rows(chunk))),
-        (FINISH, finish_chunk),
-        (RELAY, relay_chunk),
-    )
+    def total_chunk(chunk):
+        short_sum.total(chunk, short_rows(chunk))
+
+    def middle_chunk(chunk):
+        short_sum.middle(chunk, short_rows(chunk))
+
+    ahead = ((RELAY, relay_chunk), (TOTAL, total_chunk))
+    behind = ((PROJECT, project_chunk), (MIDDLE, middle_chunk), (FINISH, finish_chunk))
 
     def one_step(step, state):
+        def run(stages):
+            for lag, action in stages:
+                @pl.when(step >= lag)
+                def _():
+                    action(step - lag)
+
+        run(ahead)
         attend_chunk(step)
-        for lag, action in stages:
-            @pl.when(step >= lag)
-            def _():
-                action(step - lag)
-
+        run(behind)
         return state
 
     lax.fori_loop(0, chunks, one_step, 0)
 
-    left = {action: max(0, chunks - lag) for lag, action in stages}
-    project, total_up, middle_up, finish, relay = (action for _, action in stages)
+    left = {action: max(0, chunks - lag) for lag, action in ahead + behind}
+    left[forward_chunk] = 0
 
     def rest(action, upto):
-        for chunk in range(left[action], min(upto, chunks)):
+        upto = min(upto, FORWARDED if action is forward_chunk else chunks, chunks)
+        for chunk in range(left[action], upto):
             action(chunk)
-        left[action] = max(left[action], min(upto, chunks))
-
-    for action, upto in (
-        (total_up, chunks - 5), (project, chunks - 6), (relay, chunks - 1), (total_up, chunks - 4), (project, chunks - 5),
-        (finish, chunks - 2), (project, chunks - 4), (middle_up, chunks - 3), (relay, chunks), (finish, chunks - 1),
-        (middle_up, chunks - 2), (finish, chunks), (middle_up, chunks - 1), (total_up, chunks - 3), (middle_up, chunks),
-        (project, chunks - 3), (total_up, chunks - 2), (project, chunks - 2), (total_up, chunks - 1), (total_up, chunks),
-        (project, chunks - 1), (project, chunks),
+        left[action] = max(left[action], upto)
+
+    for action, back in (
+        (relay_chunk, 1), (total_chunk, 4), (middle_chunk, 2), (project_chunk, 4), (finish_chunk, 1), (total_chunk, 3),
+        (relay_chunk, 0), (middle_chunk, 1), (project_chunk, 3), (finish_chunk, 0), (forward_chunk, 7), (total_chunk, 2),
+        (middle_chunk, 0), (project_chunk, 2), (forward_chunk, 6), (total_chunk, 1), (project_chunk, 1),
+        (forward_chunk, 5), (total_chunk, 0), (project_chunk, 0), (forward_chunk, 0),
     ):
-        rest(action, upto)
+        rest(action, chunks - back)
 
     def wait_chunk(chunk):
         def one(source, state):
-            @pl.when(source != place)
+            @pl.when((source != place) & ((source >= forwards) | (chunk >= FORWARDED)))
             def _():
                 pair_arrival(chunk, source).wait_recv()
 
@@ -755,7 +793,16 @@
         for copy in mix_copies(chunk, mixed_rows(chunk)):
             copy.wait_send()
         short_sum.drain(chunk, short_rows(chunk))
-        for_targets(lambda target: pair_copy(chunk, target).wait_send())
+        for_targets(chunk, lambda target: pair_copy(chunk, target).wait_send())
+
+        @pl.when(chunk < FORWARDED)
+        def _():
+            def one(source, inner):
+                forward_copy(chunk, source).wait_send()
+                return inner
+
+            lax.fori_loop(0, forwards, one, 0)
+
         query_copy(chunk).wait_send()
         return state
 

time: 80.1 us -> 81.5 us (1.017)
  Pallas kernels: 79.2 us -> 80.5 us
    pallas_call x1, Pallas kernels: 79.2 us -> 80.5 us  [local(): pl.pallas_call(kernel, out_shape=jax.ShapeDtypeStruct((count, width), jnp...]
where the time goes in v4:
time: 81.5 us; the launch traced here: 81.4 us
  Pallas kernels  80.5 us (99%)
    pallas_call x1, Pallas kernels, local(): pl.pallas_call(kernel, out_shape=jax.ShapeDtypeStruct((count, width), jnp...  80.5 us

profile of v4, /device:TPU:1, one launch (start us, length us, event | category | flops | bytes accessed | tf_op | source)
XLA Modules:
  0.0 81.4 jit_solution(11166474155705792778)
XLA Ops:
  0.0 80.5 %block_kernel.1 = bf16[1024,256]{1,0:T(8,128)(2,1)S(1)} custom-call(s32[1,1024]{1,0:T(1,128)} %bitcast.4, f32[1,1024]{1,0:T(1,128)} %bitcast.5, f32[1,1024]{1,0:T(1,128)} %bitcast.6, f32[1,1024]{1,0:T(1,128)} %bitcast.7, bf16[256,1024]{1,0:T(8,128)(2,1)} %refs_4_.1, bf16[1024,256]{1,0:T(8,128)(2,1)} %refs_5_.1, bf16[1024,256]{1,0:T(8,128)(2,1)} %refs_6_.1, ...), custom_call_target="tpu_custom_call" | custom-call | tf_op jit(solution)/shard_map/block_kernel/pallas_call | solution.py:896
  80.6 0.8 copy.19

commit v5 on v4

--- a/solution.py
+++ b/solution.py
@@ -23,9 +23,8 @@
 HBM_SPEC = pl.BlockSpec(memory_space=pltpu.HBM)
 
 RELAY, FINISH, MIDDLE, TOTAL, PROJECT = (2, 2, 3, 5, 5)
-FORWARDED = 5
 STEP_KEYS = 512
-PIECES = 2
+PIECES = 4
 SET = 2
 
 
@@ -188,7 +187,6 @@
         ("queries", pltpu.VMEM((2 * rows, width // 2), low)),
         ("pair_send", dma((places, chunks))),
         ("pair_recv", dma((places, chunks))),
-        ("forward_send", dma((places, chunks))),
         ("query_send", dma((chunks,))),
         ("query_recv", dma((chunks,))),
         ("top", pltpu.VMEM((2, 1, 2 * rows), wide)),
@@ -196,8 +194,8 @@
         ("acc", pltpu.VMEM((width // 2, 2 * rows), wide)),
         ("turn", pltpu.VMEM((rows, width // 2), low)),
         ("heads_in", pltpu.VMEM((rows, width), low)),
-        ("turn_send", dma((1,))),
-        ("turn_recv", dma((1,))),
+        ("turn_send", dma((PIECES,))),
+        ("turn_recv", dma((PIECES,))),
         ("spread", pltpu.VMEM((width // 128, count, 128), wide)),
     ]
 
@@ -302,6 +300,15 @@
         s.cos_t[:, at] = cos_b * cos_k - sin_b * sin_k
         s.sin_t[:, at] = sin_b * cos_k + cos_b * sin_k
 
+    lane_f = lax.broadcasted_iota(jnp.int32, (rows, 128), 1) % HEAD_DIM
+    period_f = periods(lane_f % HALF)
+    angle_f = phase(place * rows + lax.broadcasted_iota(jnp.int32, (rows, 128), 0), period_f)
+    cos_f = jnp.cos(angle_f)
+    sin_f = jnp.where(lane_f < HALF, -jnp.sin(angle_f), jnp.sin(angle_f))
+    for block in range(lanes):
+        s.coarse_cos[:, block * 128 : block * 128 + 128] = cos_f
+        s.coarse_sin[:, block * 128 : block * 128 + 128] = sin_f
+
     pl.semaphore_wait(barrier, places + 2)
 
     def id_copy(steps):
@@ -426,25 +433,26 @@
 
     start_loads("co", "up", "down", *lift_names)
 
-    lane_slot = lax.broadcasted_iota(jnp.int32, (HEAD_DIM, LEAD), 1) // 32
-    packed = []
-    for head in range(heads):
-        rolled = pltpu.roll(s.query[head * HEAD_DIM : (head + 1) * HEAD_DIM, :LEAD].astype(jnp.float32), (32 * head + 32) % LEAD, 1)
-        packed.append(jnp.where(lane_slot == head, rolled, 0.0))
-    packed = jnp.concatenate(packed, axis=0).astype(jnp.bfloat16)
-    scores = dot(s.keys[: LEAD + WINDOW, :], packed)
-    key = lax.broadcasted_iota(jnp.int32, scores.shape, 0)
-    last = lax.broadcasted_iota(jnp.int32, scores.shape, 1) % 32 + (LEAD + WINDOW - 32)
-    floor = jnp.where(place < 2, LEAD, 0)
-    allowed = (key > last - WINDOW) & (key <= last) & (key >= floor)
-    weights, total = weigh([jnp.where(allowed, scores, masked_low)])
-    out = dot(s.values[:, : LEAD + WINDOW], weights) / total
-    unpacked = [
-        pltpu.roll(out[head * HEAD_DIM : (head + 1) * HEAD_DIM, :], (LEAD - 32 * head) % LEAD, 1) for head in range(heads)
-    ]
-    s.mixed[carry_at, :] = jnp.concatenate(unpacked, axis=0).T[32 - CARRY : 32, :].astype(jnp.bfloat16)
-    carry_copies[0].start()
-    carry_copies[1].start()
+    def attend_carry():
+        lane_slot = lax.broadcasted_iota(jnp.int32, (HEAD_DIM, LEAD), 1) // 32
+        packed = []
+        for head in range(heads):
+            rolled = pltpu.roll(s.query[head * HEAD_DIM : (head + 1) * HEAD_DIM, :LEAD].astype(jnp.float32), (32 * head + 32) % LEAD, 1)
+            packed.append(jnp.where(lane_slot == head, rolled, 0.0))
+        packed = jnp.concatenate(packed, axis=0).astype(jnp.bfloat16)
+        scores = dot(s.keys[: LEAD + WINDOW, :], packed)
+        key = lax.broadcasted_iota(jnp.int32, scores.shape, 0)
+        last = lax.broadcasted_iota(jnp.int32, scores.shape, 1) % 32 + (LEAD + WINDOW - 32)
+        floor = jnp.where(place < 2, LEAD, 0)
+        allowed = (key > last - WINDOW) & (key <= last) & (key >= floor)
+        weights, total = weigh([jnp.where(allowed, scores, masked_low)])
+        out = dot(s.values[:, : LEAD + WINDOW], weights) / total
+        unpacked = [
+            pltpu.roll(out[head * HEAD_DIM : (head + 1) * HEAD_DIM, :], (LEAD - 32 * head) % LEAD, 1) for head in range(heads)
+        ]
+        s.mixed[carry_at, :] = jnp.concatenate(unpacked, axis=0).T[32 - CARRY : 32, :].astype(jnp.bfloat16)
+        carry_copies[0].start()
+        carry_copies[1].start()
 
     part_keys = 3 * chunk_rows if span % (3 * chunk_rows) == 0 else chunk_rows
     row = lax.broadcasted_iota(jnp.int32, (chunk_rows, chunk_rows), 0)
@@ -564,15 +572,6 @@
         s.part[short_rows(chunk), :] = total
         short_sum.begin(chunk, short_rows(chunk))
 
-    lane_f = lax.broadcasted_iota(jnp.int32, (rows, 128), 1) % HEAD_DIM
-    period_f = periods(lane_f % HALF)
-    angle_f = phase(place * rows + lax.broadcasted_iota(jnp.int32, (rows, 128), 0), period_f)
-    cos_f = jnp.cos(angle_f)
-    sin_f = jnp.where(lane_f < HALF, -jnp.sin(angle_f), jnp.sin(angle_f))
-    for block in range(lanes):
-        s.coarse_cos[:, block * 128 : block * 128 + 128] = cos_f
-        s.coarse_sin[:, block * 128 : block * 128 + 128] = sin_f
-
     def pair_rows(chunk, source):
         return aligned((chunk * places + source) * group, group, group)
 
@@ -597,34 +596,17 @@
             s.query_send.at[chunk], s.query_recv.at[chunk], {"seq": cross},
         )
 
-    def for_targets(chunk, action):
+    def for_targets(action):
         def one(index, state):
             target = places - 1 - index
 
-            @pl.when((target != place) & ((target // 2 <= level + 2) | (chunk >= FORWARDED)))
+            @pl.when(target != place)
             def _():
                 action(target)
 
             return state
 
         lax.fori_loop(0, places - 2 * level, one, 0)
-
-    forwards = jnp.where(level + 1 < levels, jnp.maximum(2 * (level - 1), 0), 0)
-
-    def forward_copy(chunk, source):
-        at = pair_rows(chunk, source)
-        return remote(
-            s.pairs.at[at, :], s.pairs.at[at, :], s.forward_send.at[source, chunk], s.pair_recv.at[source, chunk],
-            {"seq": (place + 2) % places},
-        )
-
-    def forward_chunk(chunk):
-        def one(source, state):
-            pair_arrival(chunk, source).wait_recv()
-            forward_copy(chunk, source).start()
-            return state
-
-        lax.fori_loop(0, forwards, one, 0)
 
     def project_chunk(chunk):
         @pl.when(chunk == 0)
@@ -647,7 +629,7 @@
         for half in range(2):
             s.pair_out[half, at, :pair] = key[:, half * pair : half * pair + pair]
             s.pair_out[half, at, pair:] = value[:, half * pair : half * pair + pair]
-        for_targets(chunk, lambda target: pair_copy(chunk, target).start())
+        for_targets(lambda target: pair_copy(chunk, target).start())
         query = rotated(dot(coarse_in, s.cq[...]))
         for half in range(2):
             s.query_out[half, at, :] = query[:, half * pair : half * pair + pair]
@@ -673,37 +655,37 @@
 
         run(ahead)
         attend_chunk(step)
+
+        @pl.when(step == 0)
+        def _():
+            attend_carry()
+
         run(behind)
         return state
 
     lax.fori_loop(0, chunks, one_step, 0)
 
     left = {action: max(0, chunks - lag) for lag, action in ahead + behind}
-    left[forward_chunk] = 0
 
     def rest(action, upto):
-        upto = min(upto, FORWARDED if action is forward_chunk else chunks, chunks)
         for chunk in range(left[action], upto):
             action(chunk)
         left[action] = max(left[action], upto)
 
     for action, back in (
         (relay_chunk, 1), (total_chunk, 4), (middle_chunk, 2), (project_chunk, 4), (finish_chunk, 1), (total_chunk, 3),
-        (relay_chunk, 0), (middle_chunk, 1), (project_chunk, 3), (finish_chunk, 0), (forward_chunk, 7), (total_chunk, 2),
-        (middle_chunk, 0), (project_chunk, 2), (forward_chunk, 6), (total_chunk, 1), (project_chunk, 1),
-        (forward_chunk, 5), (total_chunk, 0), (project_chunk, 0), (forward_chunk, 0),
+        (relay_chunk, 0), (middle_chunk, 1), (project_chunk, 3), (finish_chunk, 0), (total_chunk, 2),
+        (middle_chunk, 0), (project_chunk, 2), (total_chunk, 1), (project_chunk, 1),
+        (total_chunk, 0), (project_chunk, 0),
     ):
         rest(action, chunks - back)
 
     def wait_chunk(chunk):
         def one(source, state):
-            @pl.when((source != place) & ((source >= forwards) | (chunk >= FORWARDED)))
-            def _():
-                pair_arrival(chunk, source).wait_recv()
-
+            pair_arrival(chunk, source).wait_recv()
             return state
 
-        lax.fori_loop(0, 2 * level + 2, one, 0)
+        lax.fori_loop(0, 2 * level, one, 0)
 
     for name in lift_names:
         loads[name].wait()
@@ -719,16 +701,56 @@
 
     def wait_queries(chunk, state):
         query_copy(chunk).wait_recv()
+        pair_arrival(chunk, cross).wait_recv()
         return state
 
     lax.fori_loop(0, chunks, wait_queries, 0)
 
-    s.top[...] = jnp.full(s.top.shape, masked_low, jnp.float32)
-    s.norm[...] = jnp.zeros(s.norm.shape, jnp.float32)
-    s.acc[...] = jnp.zeros(s.acc.shape, jnp.float32)
     per_chunk = places * group
     pair_lane = lax.broadcasted_iota(jnp.int32, (2 * rows, pair), 1) // HEAD_DIM
     queries = s.queries[...]
+    masked = [jnp.where(pair_lane == head, queries, jnp.zeros_like(queries)) for head in range(pair // HEAD_DIM)]
+
+    def absorb(block, mask, first):
+        keys, values = block[:, :pair], block[:, pair:]
+        values_t = values.astype(jnp.float32).T.astype(jnp.bfloat16)
+        for head in range(pair // HEAD_DIM):
+            scores = dot_nt(keys, masked[head])
+            pieces = [mask(begin, scores[begin : begin + group, :]) for begin in range(0, scores.shape[0], group)]
+            peak = pieces[0]
+            for piece in pieces[1:]:
+                peak = jnp.maximum(peak, piece)
+            fresh = jnp.max(peak, axis=0, keepdims=True)
+            if not first:
+                fresh = jnp.maximum(s.top[head], fresh)
+            weights = [jnp.exp2((piece - fresh) * EXP2_SCALE) for piece in pieces]
+            total = weights[0]
+            for piece in weights[1:]:
+                total = total + piece
+            total = jnp.sum(total, axis=0, keepdims=True)
+            of = slice(head * HEAD_DIM, (head + 1) * HEAD_DIM)
+            rounded = jnp.concatenate([piece.astype(jnp.bfloat16) for piece in weights], axis=0)
+            share = dot(values_t[of, :], rounded)
+            if not first:
+                factor = jnp.exp2((s.top[head] - fresh) * EXP2_SCALE)
+                total = total + s.norm[head] * factor
+                share = share + s.acc[of, :] * factor
+            s.top[head] = fresh
+            s.norm[head] = total
+            s.acc[of, :] = share
+
+    ahead_of = lax.broadcasted_iota(jnp.int32, (group, 2 * rows), 1) - lax.broadcasted_iota(
+        jnp.int32, (group, 2 * rows), 0
+    )
+
+    def own_mask(begin, piece):
+        index = begin // group
+        return jnp.where(ahead_of >= (index % 2) * rows + (index // 2) * group, piece, masked_low)
+
+    own_level = jnp.concatenate(
+        [s.pairs[aligned((chunk * places + 2 * level) * group, 2 * group, 2 * group), :] for chunk in range(chunks)], axis=0
+    )
+    absorb(own_level, own_mask, True)
 
     def key_step(step, state):
         if per_chunk <= STEP_KEYS:
@@ -741,32 +763,22 @@
             def _():
                 wait_chunk(step // ratio)
 
-        block = s.pairs[aligned(step * STEP_KEYS, STEP_KEYS, STEP_KEYS), :]
-        keys, values = block[:, :pair], block[:, pair:]
-        index = step * STEP_KEYS + lax.broadcasted_iota(jnp.int32, (STEP_KEYS, 1), 0)
-        inside = index % per_chunk
-        key_at = (inside // group) * rows + (index // per_chunk) * group + inside % group
-        query_at = 2 * level * rows + lax.broadcasted_iota(jnp.int32, (1, 2 * rows), 1)
-        allowed = key_at <= query_at
-        values_t = values.astype(jnp.float32).T.astype(jnp.bfloat16)
-        for head in range(pair // HEAD_DIM):
-            masked_q = jnp.where(pair_lane == head, queries, jnp.zeros_like(queries))
-            scores = jnp.where(allowed, dot_nt(keys, masked_q), masked_low)
-            fresh = jnp.maximum(s.top[head], jnp.max(scores, axis=0, keepdims=True))
-            factor = jnp.exp2((s.top[head] - fresh) * EXP2_SCALE)
-            weights = jnp.exp2((scores - fresh) * EXP2_SCALE)
-            s.norm[head] = s.norm[head] * factor + jnp.sum(weights, axis=0, keepdims=True)
-            of = slice(head * HEAD_DIM, (head + 1) * HEAD_DIM)
-            s.acc[of, :] = s.acc[of, :] * factor + dot(values_t[of, :], weights.astype(jnp.bfloat16))
-            s.top[head] = fresh
+        def level_mask(begin, piece):
+            source = (step * STEP_KEYS + begin) % per_chunk // group
+            return piece + jnp.where(source < 2 * level, 0.0, masked_low)
+
+        absorb(s.pairs[aligned(step * STEP_KEYS, STEP_KEYS, STEP_KEYS), :], level_mask, False)
         return state
 
     lax.fori_loop(0, places * rows // STEP_KEYS, key_step, 0)
 
-    def turn_copy():
+    size = rows // PIECES
+    at = [pl.ds(piece * size, size) for piece in range(PIECES)]
+
+    def turn_copy(piece):
         return remote(
-            s.turn, s.heads_in.at[:, aligned(side * pair, pair, pair)],
-            s.turn_send.at[0], s.turn_recv.at[0], {"seq": cross},
+            s.turn.at[at[piece], :], s.heads_in.at[at[piece], aligned(side * pair, pair, pair)],
+            s.turn_send.at[piece], s.turn_recv.at[piece], {"seq": cross},
         )
 
     def mixed_of(at):
@@ -776,7 +788,8 @@
         return jnp.concatenate(shares, axis=0).T.astype(jnp.bfloat16)
 
     s.turn[...] = mixed_of(aligned((1 - side) * rows, rows, rows))
-    turn_copy().start()
+    for piece in range(PIECES):
+        turn_copy(piece).start()
     s.heads_in[:, aligned(side * pair, pair, pair)] = mixed_of(aligned(side * rows, rows, rows))
 
     for steps in (1, 2):
@@ -793,29 +806,18 @@
         for copy in mix_copies(chunk, mixed_rows(chunk)):
             copy.wait_send()
         short_sum.drain(chunk, short_rows(chunk))
-        for_targets(chunk, lambda target: pair_copy(chunk, target).wait_send())
-
-        @pl.when(chunk < FORWARDED)
-        def _():
-            def one(source, inner):
-                forward_copy(chunk, source).wait_send()
-                return inner
-
-            lax.fori_loop(0, forwards, one, 0)
-
+        for_targets(lambda target: pair_copy(chunk, target).wait_send())
         query_copy(chunk).wait_send()
         return state
 
     lax.fori_loop(0, chunks, drain, 0)
     loads["co"].wait()
-    turn_copy().wait_recv()
 
     out_sum = HeadSum(1, peers, s.part, s.summed, buffers, s.sum_send, s.sum_recv)
     ffn_sum = HeadSum(2, peers, s.part_b, s.second, buffers, s.sum_send, s.sum_recv)
-    size = rows // PIECES
-    at = [pl.ds(piece * size, size) for piece in range(PIECES)]
 
     for piece in range(PIECES):
+        turn_copy(piece).wait_recv()
         s.part[at[piece], :] = dot(s.heads_in[at[piece], :], s.co[...])
         out_sum.begin(piece, at[piece])
     for name in ("ffn_gain", "up", "down"):
@@ -858,7 +860,8 @@
         if 0 <= step - 4 < PIECES:
             raise_rows(step - 4)
 
-    turn_copy().wait_send()
+    for piece in range(PIECES):
+        turn_copy(piece).wait_send()
     for piece in range(PIECES):
         out_sum.drain(piece, at[piece])
         ffn_sum.drain(piece, at[piece])

time: 81.5 us -> 78.2 us (0.960)
  Pallas kernels: 80.5 us -> 77.2 us
    pallas_call x1, Pallas kernels: 80.5 us -> 77.2 us  [local(): pl.pallas_call(kernel, out_shape=jax.ShapeDtypeStruct((count, width), jnp...]
where the time goes in v5:
time: 78.2 us; the launch traced here: 78.1 us
  Pallas kernels  77.2 us (99%)
  local copies, waits for them, and re-layouts  0.8 us (1%)
    pallas_call x1, Pallas kernels, local(): pl.pallas_call(kernel, out_shape=jax.ShapeDtypeStruct((count, width), jnp...  77.2 us

profile of v5, /device:TPU:1, one launch (start us, length us, event | category | flops | bytes accessed | tf_op | source)
XLA Modules:
  0.0 78.1 jit_solution(4932951920402861381)
XLA Ops:
  0.0 77.2 %block_kernel.1 = bf16[1024,256]{1,0:T(8,128)(2,1)S(1)} custom-call(s32[1,1024]{1,0:T(1,128)} %bitcast.4, f32[1,1024]{1,0:T(1,128)} %bitcast.5, f32[1,1024]{1,0:T(1,128)} %bitcast.6, f32[1,1024]{1,0:T(1,128)} %bitcast.7, bf16[256,1024]{1,0:T(8,128)(2,1)} %refs_4_.1, bf16[1024,256]{1,0:T(8,128)(2,1)} %refs_5_.1, bf16[1024,256]{1,0:T(8,128)(2,1)} %refs_6_.1, ...), custom_call_target="tpu_custom_call" | custom-call | tf_op jit(solution)/shard_map/block_kernel/pallas_call | solution.py:899
  77.3 0.8 %copy.19 = bf16[1024,256]{1,0:T(8,128)(2,1)} copy(bf16[1024,256]{1,0:T(8,128)(2,1)S(1)} %block_kernel.1) | data formatting | bytes 1048576

commit v6 on v5

--- a/solution.py
+++ b/solution.py
@@ -23,7 +23,7 @@
 HBM_SPEC = pl.BlockSpec(memory_space=pltpu.HBM)
 
 RELAY, FINISH, MIDDLE, TOTAL, PROJECT = (2, 2, 3, 5, 5)
-STEP_KEYS = 512
+STEP_KEYS = 256
 PIECES = 4
 SET = 2
 
@@ -637,6 +637,19 @@
         s.pairs[pair_rows(chunk, place), :] = s.pair_out[side, at, :]
         s.queries[aligned(side * rows + chunk * group, group, group), :] = s.query_out[side, at, :]
 
+    def lay_out():
+        for name in lift_names:
+            loads[name].wait()
+        part_rows = count // SHORTEN
+        for block in range(lanes):
+            for begin in range(0, full, part_rows):
+                flat = s.raw.at[block, pl.ds(begin, part_rows)].reshape(part_rows * SHORTEN, 128)
+                s.spread[block] = flat[...].astype(jnp.float32)
+                for member in range(SHORTEN):
+                    s.lift[begin : begin + part_rows, member * width + block * 128 : member * width + block * 128 + 128] = (
+                        s.spread[block, pl.ds(member, part_rows, stride=SHORTEN), :].astype(jnp.bfloat16)
+                    )
+
     def total_chunk(chunk):
         short_sum.total(chunk, short_rows(chunk))
 
@@ -676,9 +689,11 @@
         (relay_chunk, 1), (total_chunk, 4), (middle_chunk, 2), (project_chunk, 4), (finish_chunk, 1), (total_chunk, 3),
         (relay_chunk, 0), (middle_chunk, 1), (project_chunk, 3), (finish_chunk, 0), (total_chunk, 2),
         (middle_chunk, 0), (project_chunk, 2), (total_chunk, 1), (project_chunk, 1),
-        (total_chunk, 0), (project_chunk, 0),
     ):
         rest(action, chunks - back)
+    lay_out()
+    rest(total_chunk, chunks)
+    rest(project_chunk, chunks)
 
     def wait_chunk(chunk):
         def one(source, state):
@@ -686,18 +701,6 @@
             return state
 
         lax.fori_loop(0, 2 * level, one, 0)
-
-    for name in lift_names:
-        loads[name].wait()
-    part_rows = count // SHORTEN
-    for block in range(lanes):
-        for begin in range(0, full, part_rows):
-            flat = s.raw.at[block, pl.ds(begin, part_rows)].reshape(part_rows * SHORTEN, 128)
-            s.spread[block] = flat[...].astype(jnp.float32)
-            for member in range(SHORTEN):
-                s.lift[begin : begin + part_rows, member * width + block * 128 : member * width + block * 128 + 128] = (
-                    s.spread[block, pl.ds(member, part_rows, stride=SHORTEN), :].astype(jnp.bfloat16)
-                )
 
     def wait_queries(chunk, state):
         query_copy(chunk).wait_recv()

time: 78.2 us -> 80.8 us (1.033)
  Pallas kernels: 77.2 us -> 79.9 us
    pallas_call x1, Pallas kernels: 77.2 us -> 79.9 us  [local(): pl.pallas_call(kernel, out_shape=jax.ShapeDtypeStruct((count, width), jnp...]
where the time goes in v6:
time: 80.8 us; the launch traced here: 80.7 us
  Pallas kernels  79.9 us (99%)
    pallas_call x1, Pallas kernels, local(): pl.pallas_call(kernel, out_shape=jax.ShapeDtypeStruct((count, width), jnp...  79.9 us

profile of v6, /device:TPU:1, one launch (start us, length us, event | category | flops | bytes accessed | tf_op | source)
XLA Modules:
  0.0 80.7 jit_solution(18147523188273136999)
XLA Ops:
  0.0 79.9 %block_kernel.1 = bf16[1024,256]{1,0:T(8,128)(2,1)S(1)} custom-call(s32[1,1024]{1,0:T(1,128)} %bitcast.4, f32[1,1024]{1,0:T(1,128)} %bitcast.5, f32[1,1024]{1,0:T(1,128)} %bitcast.6, f32[1,1024]{1,0:T(1,128)} %bitcast.7, bf16[256,1024]{1,0:T(8,128)(2,1)} %refs_4_.1, bf16[1024,256]{1,0:T(8,128)(2,1)} %refs_5_.1, bf16[1024,256]{1,0:T(8,128)(2,1)} %refs_6_.1, ...), custom_call_target="tpu_custom_call" | custom-call | tf_op jit(solution)/shard_map/block_kernel/pallas_call | solution.py:902
  79.9 0.8 copy.19

commit v7 on v5

--- a/solution.py
+++ b/solution.py
@@ -23,7 +23,7 @@
 HBM_SPEC = pl.BlockSpec(memory_space=pltpu.HBM)
 
 RELAY, FINISH, MIDDLE, TOTAL, PROJECT = (2, 2, 3, 5, 5)
-STEP_KEYS = 512
+STEP_KEYS = 1024
 PIECES = 4
 SET = 2
 
@@ -687,18 +687,6 @@
 
         lax.fori_loop(0, 2 * level, one, 0)
 
-    for name in lift_names:
-        loads[name].wait()
-    part_rows = count // SHORTEN
-    for block in range(lanes):
-        for begin in range(0, full, part_rows):
-            flat = s.raw.at[block, pl.ds(begin, part_rows)].reshape(part_rows * SHORTEN, 128)
-            s.spread[block] = flat[...].astype(jnp.float32)
-            for member in range(SHORTEN):
-                s.lift[begin : begin + part_rows, member * width + block * 128 : member * width + block * 128 + 128] = (
-                    s.spread[block, pl.ds(member, part_rows, stride=SHORTEN), :].astype(jnp.bfloat16)
-                )
-
     def wait_queries(chunk, state):
         query_copy(chunk).wait_recv()
         pair_arrival(chunk, cross).wait_recv()
@@ -792,25 +780,18 @@
         turn_copy(piece).start()
     s.heads_in[:, aligned(side * pair, pair, pair)] = mixed_of(aligned(side * rows, rows, rows))
 
-    for steps in (1, 2):
-        @pl.when(place + steps < places)
-        def _():
-            id_copy(steps).wait_send()
-
-    for copy in column_copies:
-        copy.wait_send()
-    for copy in carry_copies:
-        copy.wait_send()
-
-    def drain(chunk, state):
-        for copy in mix_copies(chunk, mixed_rows(chunk)):
-            copy.wait_send()
-        short_sum.drain(chunk, short_rows(chunk))
-        for_targets(lambda target: pair_copy(chunk, target).wait_send())
-        query_copy(chunk).wait_send()
-        return state
-
-    lax.fori_loop(0, chunks, drain, 0)
+    for name in lift_names:
+        loads[name].wait()
+    part_rows = count // SHORTEN
+    for block in range(lanes):
+        for begin in range(0, full, part_rows):
+            flat = s.raw.at[block, pl.ds(begin, part_rows)].reshape(part_rows * SHORTEN, 128)
+            s.spread[block] = flat[...].astype(jnp.float32)
+            for member in range(SHORTEN):
+                s.lift[begin : begin + part_rows, member * width + block * 128 : member * width + block * 128 + 128] = (
+                    s.spread[block, pl.ds(member, part_rows, stride=SHORTEN), :].astype(jnp.bfloat16)
+                )
+
     loads["co"].wait()
 
     out_sum = HeadSum(1, peers, s.part, s.summed, buffers, s.sum_send, s.sum_recv)
@@ -824,6 +805,25 @@
         loads[name].wait()
     for piece in range(PIECES):
         out_sum.middle(piece, at[piece])
+    for steps in (1, 2):
+        @pl.when(place + steps < places)
+        def _():
+            id_copy(steps).wait_send()
+
+    for copy in column_copies:
+        copy.wait_send()
+    for copy in carry_copies:
+        copy.wait_send()
+
+    def drain(chunk, state):
+        for copy in mix_copies(chunk, mixed_rows(chunk)):
+            copy.wait_send()
+        short_sum.drain(chunk, short_rows(chunk))
+        for_targets(lambda target: pair_copy(chunk, target).wait_send())
+        query_copy(chunk).wait_send()
+        return state
+
+    lax.fori_loop(0, chunks, drain, 0)
 
     def feed(piece):
         out_sum.end(piece, at[piece])

time: 78.2 us -> 77.4 us (0.990)
  Pallas kernels: 77.2 us -> 76.4 us
    pallas_call x1, Pallas kernels: 77.2 us -> 76.4 us  [local(): pl.pallas_call(kernel, out_shape=jax.ShapeDtypeStruct((count, width), jnp...]
where the time goes in v7:
time: 77.4 us; the launch traced here: 77.2 us
  Pallas kernels  76.4 us (99%)
  local copies, waits for them, and re-layouts  0.8 us (1%)
    pallas_call x1, Pallas kernels, local(): pl.pallas_call(kernel, out_shape=jax.ShapeDtypeStruct((count, width), jnp...  76.4 us

profile of v7, /device:TPU:1, one launch (start us, length us, event | category | flops | bytes accessed | tf_op | source)
XLA Modules:
  0.0 77.2 jit_solution(8407257458686952675)
XLA Ops:
  0.0 76.4 %block_kernel.1 = bf16[1024,256]{1,0:T(8,128)(2,1)S(1)} custom-call(s32[1,1024]{1,0:T(1,128)} %bitcast.4, f32[1,1024]{1,0:T(1,128)} %bitcast.5, f32[1,1024]{1,0:T(1,128)} %bitcast.6, f32[1,1024]{1,0:T(1,128)} %bitcast.7, bf16[256,1024]{1,0:T(8,128)(2,1)} %refs_4_.1, bf16[1024,256]{1,0:T(8,128)(2,1)} %refs_5_.1, bf16[1024,256]{1,0:T(8,128)(2,1)} %refs_6_.1, ...), custom_call_target="tpu_custom_call" | custom-call | tf_op jit(solution)/shard_map/block_kernel/pallas_call | solution.py:899
  76.4 0.8 %copy.19 = bf16[1024,256]{1,0:T(8,128)(2,1)} copy(bf16[1024,256]{1,0:T(8,128)(2,1)S(1)} %block_kernel.1) | data formatting | bytes 1048576

commit v8 on v7

--- a/solution.py
+++ b/solution.py
@@ -762,6 +762,7 @@
 
     size = rows // PIECES
     at = [pl.ds(piece * size, size) for piece in range(PIECES)]
+    wide = [pl.ds(2 * half * size, 2 * size) for half in range(PIECES // 2)]
 
     def turn_copy(piece):
         return remote(
@@ -827,11 +828,14 @@
 
     def feed(piece):
         out_sum.end(piece, at[piece])
-        value = s.short[at[piece], :].astype(jnp.float32) + s.summed[at[piece], :].astype(jnp.float32)
-        s.first[at[piece], :] = value
+        out_sum.end(piece + 1, at[piece + 1])
+        half = wide[piece // 2]
+        value = s.short[half, :].astype(jnp.float32) + s.summed[half, :].astype(jnp.float32)
+        s.first[half, :] = value
         inner = jax.nn.gelu(dot(normed(value, s.ffn_gain[...]), s.up[...])).astype(jnp.bfloat16)
-        s.part_b[at[piece], :] = dot(inner, s.down[...])
+        s.part_b[half, :] = dot(inner, s.down[...])
         ffn_sum.begin(piece, at[piece])
+        ffn_sum.begin(piece + 1, at[piece + 1])
 
     def raise_rows(piece):
         ffn_sum.end(piece, at[piece])
@@ -848,17 +852,21 @@
                 s.stream[block, base_at, :] + s.spread[block, to, :]
             ).astype(jnp.bfloat16)
 
-    for step in range(PIECES + 4):
-        if step < PIECES:
-            out_sum.total(step, at[step])
-        if 0 <= step - 1 < PIECES:
-            feed(step - 1)
-        if 0 <= step - 2 < PIECES:
-            ffn_sum.middle(step - 2, at[step - 2])
-        if 0 <= step - 3 < PIECES:
-            ffn_sum.total(step - 3, at[step - 3], s.first)
-        if 0 <= step - 4 < PIECES:
-            raise_rows(step - 4)
+    def out_total(piece):
+        out_sum.total(piece, at[piece])
+
+    def ffn_middle(piece):
+        ffn_sum.middle(piece, at[piece])
+
+    def ffn_total(piece):
+        ffn_sum.total(piece, at[piece], s.first)
+
+    for action, piece in (
+        (out_total, 0), (out_total, 1), (feed, 0), (out_total, 2), (ffn_middle, 0), (out_total, 3), (ffn_middle, 1),
+        (feed, 2), (ffn_middle, 2), (ffn_middle, 3), (ffn_total, 0), (ffn_total, 1), (raise_rows, 0), (ffn_total, 2),
+        (raise_rows, 1), (ffn_total, 3), (raise_rows, 2), (raise_rows, 3),
+    ):
+        action(piece)
 
     for piece in range(PIECES):
         turn_copy(piece).wait_send()

time: 77.4 us -> 76.3 us (0.986)
  Pallas kernels: 76.4 us -> 75.4 us
    pallas_call x1, Pallas kernels: 76.4 us -> 75.4 us  [local(): pl.pallas_call(kernel, out_shape=jax.ShapeDtypeStruct((count, width), jnp...]
where the time goes in v8:
time: 76.3 us; the launch traced here: 76.2 us
  Pallas kernels  75.4 us (99%)
  local copies, waits for them, and re-layouts  0.8 us (1%)
    pallas_call x1, Pallas kernels, local(): pl.pallas_call(kernel, out_shape=jax.ShapeDtypeStruct((count, width), jnp...  75.4 us

profile of v8, /device:TPU:1, one launch (start us, length us, event | category | flops | bytes accessed | tf_op | source)
XLA Modules:
  0.0 76.2 jit_solution(5538542202897691896)
XLA Ops:
  0.0 75.4 %block_kernel.1 = bf16[1024,256]{1,0:T(8,128)(2,1)S(1)} custom-call(s32[1,1024]{1,0:T(1,128)} %bitcast.4, f32[1,1024]{1,0:T(1,128)} %bitcast.5, f32[1,1024]{1,0:T(1,128)} %bitcast.6, f32[1,1024]{1,0:T(1,128)} %bitcast.7, bf16[256,1024]{1,0:T(8,128)(2,1)} %refs_4_.1, bf16[1024,256]{1,0:T(8,128)(2,1)} %refs_5_.1, bf16[1024,256]{1,0:T(8,128)(2,1)} %refs_6_.1, ...), custom_call_target="tpu_custom_call" | custom-call | tf_op jit(solution)/shard_map/block_kernel/pallas_call | solution.py:907
  75.4 0.8 %copy.19 = bf16[1024,256]{1,0:T(8,128)(2,1)} copy(bf16[1024,256]{1,0:T(8,128)(2,1)S(1)} %block_kernel.1) | data formatting | bytes 1048576
